TPU v7x, 128 devices: a whole 4x4x4 slice. The times are simulated.
128 devices in a mesh: row: 16 (over x_lo, y, core), col: 8 (over z, x_hi).
Axes of the slice: x: 4 (x_hi: 2, x_lo: 2; x = x_hi * 2 + x_lo), y: 4, z: 4, core: 2. Of those that a mesh axis runs over, the one named last changes fastest.
Arguments:
- surface_height: float32 [2048, 2048], P('row', 'col'), may hold values from -1.2 to 1.2
- surface_potential: float32 [2048, 2048], P('row', 'col'), may hold values from -4 to 4
- velocity: float32 [3, 16, 1024, 1024], P(None, None, 'row', 'col'), may hold values from -1.25 to 1.25
Outputs:
- height_rate: float32 [2048, 2048], P('row', 'col')
- potential_rate: float32 [2048, 2048], P('row', 'col')
- velocity_next: float32 [3, 16, 1024, 1024], P(None, None, 'row', 'col')
All inputs are finite; a program needn't handle non-finite values.
Results may differ from a plain program's by a relative error of at most 0.00019.
Values sent between devices are 32-bit elements; how exact they have to be, the bound alone decides.
A program may use at most 128 MiB of HBM per device.

v0:
```python
import jax
import jax.numpy as jnp
from jax import lax
from jax.sharding import Mesh
from jax.sharding import PartitionSpec as P

NX = 2048
NY = 2048
COARSE = 2
COL = ("col_0", "col_1")
ROW_COL = ("row", "col_0", "col_1")


GRAVITY = 1.0
SURFACE_STEP = 0.05
FLOW_STEP = 0.5
VISCOSITY = 0.2
DECAY_RATE = 0.05


def in_one_piece(arrays, axis, split_dim, concat_dim, along):
    both = jnp.concatenate(arrays, axis=along)
    whole, at, done = (
        lax.all_to_all(both, axis, split_axis=split_dim, concat_axis=concat_dim, tiled=True),
        0,
        [],
    )
    for a in arrays:
        done.append(lax.slice_in_dim(whole, at, at + a.shape[along], axis=along))
        at += a.shape[along]
    return tuple(done)


def cut_along(x, dim, peers):
    dims = x.shape
    pieces = x.reshape(*dims[:dim], peers, dims[dim] // peers, *dims[dim + 1 :])
    return jnp.moveaxis(pieces, dim, 0)


def joined_along(pieces, dim):
    pieces = jnp.moveaxis(pieces, 0, dim)
    dims = pieces.shape
    return pieces.reshape(*dims[:dim], dims[dim] * dims[dim + 1], *dims[dim + 2 :])


def exchange_in_order(pieces, axes, order):
    dims = [lax.axis_size(a) for a in axes]
    pieces = pieces.reshape(*dims, *pieces.shape[1:])
    for k in order:
        pieces = lax.all_to_all(pieces, axes[k], split_axis=k, concat_axis=k, tiled=True)
    return pieces.reshape(-1, *pieces.shape[len(axes) :])


def one_axis_at_a_time(x, axes, order, split_dim, concat_dim):
    pieces = cut_along(x, split_dim, lax.axis_size(axes))
    return joined_along(exchange_in_order(pieces, axes, order), concat_dim)


def with_halo(x, sides, width):
    edges = {}
    for axis, dim in sides:
        peers, length = (lax.axis_size(axis), x.shape[dim])
        up = [(i, (i + 1) % peers) for i in range(peers)]
        last = lax.slice_in_dim(x, length - width, length, axis=dim)
        leading = lax.slice_in_dim(x, 0, width, axis=dim)
        edges[dim] = (
            lax.ppermute(last, axis, up),
            lax.ppermute(leading, axis, [(b, a) for a, b in up]),
        )
    done = []
    for _, dim in sides:
        low, high = edges[dim]
        around = [(width, width) if d in done else (0, 0) for d in range(x.ndim)]
        x = jnp.concatenate([jnp.pad(low, around), x, jnp.pad(high, around)], axis=dim)
        done.append(dim)
    return x


def wave_numbers(index, length):
    signed = jnp.where(index < length // 2, index, index - length)
    kept_mask = (jnp.abs(signed) <= length // 3).astype(jnp.float32)
    return (2.0 * jnp.pi / length * signed.astype(jnp.float32), kept_mask)


def coarsen(source):
    rows_out = source.shape[0] // COARSE
    cols_out = source.shape[1] // COARSE
    return source.reshape(rows_out, COARSE, cols_out, COARSE).mean(axis=(1, 3))


def flow_update(padded_flow, padded_load, surface_u, surface_v):
    depth_count = padded_flow.shape[1]
    level_mid = jnp.arange(depth_count, dtype=jnp.float32)[:, None, None] + 0.5
    drift_decay = jnp.exp(-2.0 * DECAY_RATE * level_mid)
    load_decay = jnp.exp(-DECAY_RATE * level_mid)

    def derivs(source, top_value):
        middle = source[:, 1:-1, 1:-1]
        above_cell = jnp.concatenate([top_value[None], middle[:-1]], axis=0)
        below_cell = jnp.concatenate([middle[1:], middle[-1:]], axis=0)
        east_side = source[:, 1:-1, 2:]
        west_side = source[:, 1:-1, :-2]
        north_side = source[:, 2:, 1:-1]
        south_side = source[:, :-2, 1:-1]
        laplace = (
            east_side + west_side + north_side + south_side + above_cell + below_cell - 6.0 * middle
        )
        return (
            middle,
            0.5 * (east_side - west_side),
            0.5 * (north_side - south_side),
            0.5 * (above_cell - below_cell),
            laplace,
        )

    u_mid, u_dx, u_dy, u_dz, u_lap = derivs(padded_flow[0], surface_u)
    v_mid, v_dx, v_dy, v_dz, v_lap = derivs(padded_flow[1], surface_v)
    w_mid, w_dx, w_dy, w_dz, w_lap = derivs(padded_flow[2], jnp.zeros_like(surface_u))
    vort_x = w_dy - v_dz
    vort_y = u_dz - w_dx
    vort_z = v_dx - u_dy
    drift_u = surface_u[None] * drift_decay
    drift_v = surface_v[None] * drift_decay
    load_x = 0.5 * (padded_load[1:-1, 2:] - padded_load[1:-1, :-2])[None] * load_decay
    load_y = 0.5 * (padded_load[2:, 1:-1] - padded_load[:-2, 1:-1])[None] * load_decay

    def advance(middle, slope_x, slope_y, slope_z, laplace, forcing):
        carried = u_mid * slope_x + v_mid * slope_y + w_mid * slope_z
        return middle + FLOW_STEP * (-carried + VISCOSITY * laplace + forcing)

    next_u = advance(u_mid, u_dx, u_dy, u_dz, u_lap, drift_v * vort_z - load_x)
    next_v = advance(v_mid, v_dx, v_dy, v_dz, v_lap, -drift_u * vort_z - load_y)
    next_w = advance(w_mid, w_dx, w_dy, w_dz, w_lap, drift_u * vort_y - drift_v * vort_x)
    return jnp.stack([next_u, next_v, next_w])


def product(form, left, right):
    return jnp.einsum(form, left, right, precision=lax.Precision.HIGHEST)


def complex_product(form, left_real, left_imag, right_real, right_imag):
    if left_imag is None:
        return (product(form, left_real, right_real), product(form, left_real, right_imag))
    out_real = product(form, left_real, right_real) - product(form, left_imag, right_imag)
    out_imag = product(form, left_real, right_imag) + product(form, left_imag, right_real)
    return (out_real, out_imag)


def tables(length, direction):
    index = jnp.arange(length, dtype=jnp.int32)
    angle = 2.0 * jnp.pi / length * (index[:, None] * index[None, :] % length).astype(jnp.float32)
    return (jnp.cos(angle), direction * jnp.sin(angle))


def twiddles(factor_one, factor_two, direction):
    total = factor_one * factor_two
    index_one = jnp.arange(factor_one, dtype=jnp.int32)
    index_two = jnp.arange(factor_two, dtype=jnp.int32)
    angle = (
        2.0 * jnp.pi / total * (index_one[:, None] * index_two[None, :] % total).astype(jnp.float32)
    )
    return (jnp.cos(angle), direction * jnp.sin(angle))


def transform(real_part, imag_part, direction, layout, real_only):
    if layout == "back":
        length = real_part.shape[1]
    else:
        length = real_part.shape[2]
    factor_one = 1 << (length.bit_length() - 1) // 2
    factor_two = length // factor_one
    cos_one, sin_one = tables(factor_one, direction)
    cos_two, sin_two = tables(factor_two, direction)
    twist_cos, twist_sin = twiddles(factor_one, factor_two, direction)
    batch_size = real_part.shape[0]
    if layout == "back":
        cross_len = real_part.shape[2]
        shape_four = (batch_size, factor_one, factor_two, cross_len)
        first_form = "banm,ak->bknm"
        second_form = "bknm,nq->bmqk"
        twist_cos = twist_cos[None, :, :, None]
        twist_sin = twist_sin[None, :, :, None]
        out_shape = (batch_size, cross_len, length)
    else:
        cross_len = real_part.shape[1]
        shape_four = (batch_size, cross_len, factor_one, factor_two)
        first_form = "bman,ak->bmkn"
        twist_cos = twist_cos[None, None]
        twist_sin = twist_sin[None, None]
        if layout == "front":
            second_form = "bmkn,nq->bqkm"
            out_shape = (batch_size, length, cross_len)
        else:
            second_form = "bmkn,nq->bmqk"
            out_shape = (batch_size, cross_len, length)
    left_real = real_part.reshape(shape_four)
    left_imag = None if imag_part is None else imag_part.reshape(shape_four)
    mid_real, mid_imag = complex_product(first_form, left_real, left_imag, cos_one, sin_one)
    turned_real = mid_real * twist_cos - mid_imag * twist_sin
    turned_imag = mid_real * twist_sin + mid_imag * twist_cos
    if real_only:
        result = product(second_form, turned_real, cos_two) - product(
            second_form, turned_imag, sin_two
        )
        return result.reshape(out_shape)
    out_real, out_imag = complex_product(second_form, turned_real, turned_imag, cos_two, sin_two)
    return (out_real.reshape(out_shape), out_imag.reshape(out_shape))


def scaled(pair_value, factor):
    return (pair_value[0] * factor, pair_value[1] * factor)


def turned(pair_value, factor):
    return (-factor * pair_value[1], factor * pair_value[0])


def unfold_half(full_real, full_imag, kept_modes):
    weights = jnp.where(jnp.arange(kept_modes, dtype=jnp.int32) == 0, 1.0, 2.0).astype(jnp.float32)[
        None, :, None
    ]
    padding = jnp.zeros((full_real.shape[0], NX - kept_modes, full_real.shape[2]), jnp.float32)
    return (
        jnp.concatenate([full_real * weights, padding], axis=1),
        jnp.concatenate([full_imag * weights, padding], axis=1),
    )


def local(surface_height, surface_potential, velocity):
    col_count = lax.axis_size(COL)
    device_count = lax.axis_size("row") * col_count
    place = lax.axis_index("row") * col_count + lax.axis_index(COL)
    kept_modes = (NX // 3 + device_count) // device_count * device_count
    modes_each = kept_modes // device_count
    kx_index = place * modes_each + jnp.arange(modes_each, dtype=jnp.int32)
    kx_values, kx_kept = wave_numbers(kx_index, NX)
    ky_values, ky_kept = wave_numbers(jnp.arange(NY, dtype=jnp.int32), NY)
    kx_grid = kx_values[:, None]
    ky_grid = ky_values[None, :]
    mask = kx_kept[:, None] * ky_kept[None, :]
    magnitude = jnp.sqrt(kx_grid * kx_grid + ky_grid * ky_grid)

    def forward(stacked):
        pencil = lax.all_to_all(stacked, COL, split_axis=1, concat_axis=2, tiled=True)
        wide_real, wide_imag = transform(pencil, None, -1.0, "front", False)
        slab_real, slab_imag = in_one_piece(
            (wide_real[:, :kept_modes], wide_imag[:, :kept_modes]), ROW_COL, 1, 2, 0
        )
        spec_real, spec_imag = transform(slab_real, slab_imag, -1.0, "last", False)
        return (spec_real * mask, spec_imag * mask)

    def inverse(pair_list):
        spec_real = jnp.stack([pair_item[0] for pair_item in pair_list])
        spec_imag = jnp.stack([pair_item[1] for pair_item in pair_list])
        line_real, line_imag = transform(spec_real, spec_imag, 1.0, "last", False)
        full_real, full_imag = in_one_piece((line_real, line_imag), ROW_COL, 2, 1, 0)
        full_real, full_imag = unfold_half(full_real, full_imag, kept_modes)
        pencil = transform(full_real, full_imag, 1.0, "back", True) / float(NX * NY)
        return one_axis_at_a_time(pencil, COL, (0, 1), 2, 1)

    first_real, first_imag = forward(jnp.stack([surface_potential, surface_height]))
    pot_hat = (first_real[0], first_imag[0])
    height_hat = (first_real[1], first_imag[1])
    first_fields = inverse(
        [
            scaled(pot_hat, magnitude),
            scaled(pot_hat, magnitude * magnitude),
            scaled(pot_hat, magnitude * magnitude * magnitude),
            turned(pot_hat, kx_grid),
            turned(pot_hat, ky_grid),
            turned(height_hat, kx_grid),
            turned(height_hat, ky_grid),
        ]
    )
    vert_one = first_fields[0]
    curve_one = first_fields[1]
    cube_one = first_fields[2]
    pot_dx = first_fields[3]
    pot_dy = first_fields[4]
    height_dx = first_fields[5]
    height_dy = first_fields[6]
    second_pot = -surface_height * vert_one
    second_real, second_imag = forward(second_pot[None])
    second_hat = (second_real[0], second_imag[0])
    second_fields = inverse(
        [scaled(second_hat, magnitude), scaled(second_hat, magnitude * magnitude)]
    )
    vert_two = second_fields[0]
    curve_two = second_fields[1]
    third_pot = -surface_height * vert_two - 0.5 * surface_height * surface_height * curve_one
    third_real, third_imag = forward(third_pot[None])
    vert_three = inverse([scaled((third_real[0], third_imag[0]), magnitude)])[0]
    vertical = (
        vert_one
        + vert_two
        + vert_three
        + surface_height * (curve_one + curve_two)
        + 0.5 * surface_height * surface_height * cube_one
    )
    slope = height_dx * height_dx + height_dy * height_dy
    height_rate = -(height_dx * pot_dx + height_dy * pot_dy) + (1.0 + slope) * vertical
    potential_rate = (
        -GRAVITY * surface_height
        - 0.5 * (pot_dx * pot_dx + pot_dy * pot_dy)
        + 0.5 * (1.0 + slope) * vertical * vertical
    )
    pressure = GRAVITY * coarsen(surface_height + SURFACE_STEP * height_rate)
    surface_u = coarsen(pot_dx)
    surface_v = coarsen(pot_dy)
    depth_count = velocity.shape[1]
    stacked_block = jnp.concatenate(
        [velocity.reshape((3 * depth_count,) + velocity.shape[2:]), pressure[None]], axis=0
    )
    padded_block = with_halo(stacked_block, (("row", 1), (COL, 2)), 1)
    padded_flow = padded_block[:-1].reshape((3, depth_count) + padded_block.shape[1:])
    padded_load = padded_block[-1]
    velocity_next = flow_update(padded_flow, padded_load, surface_u, surface_v)
    return (height_rate, potential_rate, velocity_next)


def solution(mesh):
    torus = Mesh(mesh.devices.reshape(mesh.shape["row"], 4, 2), ("row", "col_0", "col_1"))
    in_specs = (P("row", COL), P("row", COL), P(None, None, "row", COL))
    out_specs = (P("row", COL), P("row", COL), P(None, None, "row", COL))
    return jax.shard_map(local, mesh=torus, in_specs=in_specs, out_specs=out_specs, check_vma=False)
```

profile of v0, /device:TPU:1, one launch (start us, length us, event | category | flops | bytes accessed | tf_op | source)
XLA Modules:
  0.0 496.9 jit_solution(10821120104185174683)
XLA Ops:
  3.6 8.3 %all-to-all-start = ((f32[2,128,256]{2,0,1:T(2,128)}), f32[2,128,256]{2,0,1:T(2,128)S(1)}, u32[]{:S(2)}, u32[]{:S(2)}) async-start(f32[2,128,256]{2,0,1:T(2,128)} %pad_maximum_fusion.28), calls=%async_computation | async-start | bytes 524288 | tf_op jit(solution)/shard_map/all_to_all | solution.py:244
  12.6 6.9 %all-to-all-done = f32[2,128,256]{2,0,1:T(2,128)S(1)} async-done(((f32[2,128,256]{2,0,1:T(2,128)}), f32[2,128,256]{2,0,1:T(2,128)S(1)}, u32[]{:S(2)}, u32[]{:S(2)}) %all-to-all-start) | async-done | bytes 262176 | tf_op jit(solution)/shard_map/all_to_all | solution.py:244
  28.3 7.3 %all-to-all-start.1 = ((f32[128,1,384]{2,1,0:T(1,128)}), f32[128,1,384]{2,1,0:T(1,128)S(1)}, u32[]{:S(2)}, u32[]{:S(2)}) async-start(f32[128,1,384]{2,1,0:T(1,128)} %reshape.1260), calls=%async_computation.1 | async-start | bytes 393216 | tf_op jit(solution)/shard_map/all_to_all | solution.py:24
  35.7 9.8 %all-to-all-done.1 = f32[128,1,384]{2,1,0:T(1,128)S(1)} async-done(((f32[128,1,384]{2,1,0:T(1,128)}), f32[128,1,384]{2,1,0:T(1,128)S(1)}, u32[]{:S(2)}, u32[]{:S(2)}) %all-to-all-start.1) | async-done | bytes 196640 | tf_op jit(solution)/shard_map/all_to_all | solution.py:24
  74.6 7.6 %reshape.1262 = f32[128,1,1344]{2,1,0:T(1,128)} reshape(f32[2048,6,14]{2,1,0:T(8,128)} %bitcast.790) | data formatting | bytes 1376256
  87.0 14.7 %all-to-all-done.2 = f32[128,1,1344]{2,1,0:T(1,128)S(1)} async-done(((f32[128,1,1344]{2,1,0:T(1,128)}), f32[128,1,1344]{2,1,0:T(1,128)S(1)}, u32[]{:S(2)}, u32[]{:S(2)}) %all-to-all-start.2) | async-done | bytes 688160 | tf_op jit(solution)/shard_map/all_to_all | solution.py:24
  103.9 6.5 %reshape.1263 = f32[2048,6,14]{2,1,0:T(8,128)} reshape(f32[128,1344]{1,0:T(8,128)S(1)} %reduce.29) | data formatting | bytes 1376256
  110.4 9.8 %copy.315 = f32[14,6,128,16]{3,2,0,1:T(8,128)} copy(f32[14,6,128,16]{0,1,3,2:T(8,128)} %bitcast.791) | data formatting | bytes 1376256 | tf_op jit(solution)/shard_map/all_to_all | solution.py:24
  171.1 14.8 %all_to_all.165 = f32[4,2,7,16,256]{4,1,3,2,0:T(2,128)S(1)} all-to-all(f32[4,2,7,16,256]{4,1,3,2,0:T(2,128)S(1)} %copy.261), channel_id=1, replica_groups=mesh['row'=16,'col_0'=4,'col_1'=2] {'col_0'}, dimensions={0} | all-to-all | bytes 1835008 | tf_op jit(solution)/shard_map/all_to_all | solution.py:50
  186.5 13.5 %all_to_all.166 = f32[4,2,7,16,256]{4,0,3,2,1:T(4,128)S(1)} all-to-all(f32[4,2,7,16,256]{4,0,3,2,1:T(4,128)S(1)} %copy.262), channel_id=1, replica_groups=mesh['row'=16,'col_0'=4,'col_1'=2] {'col_1'}, dimensions={1} | all-to-all | bytes 1835008 | tf_op jit(solution)/shard_map/all_to_all | solution.py:50
  205.5 6.9 %all-to-all-done.5 = f32[1,128,256]{2,0,1:T(1,128)S(1)} async-done(((f32[1,128,256]{2,0,1:T(1,128)}), f32[1,128,256]{2,0,1:T(1,128)S(1)}, u32[]{:S(2)}, u32[]{:S(2)}) %all-to-all-start.5) | async-done | bytes 131104 | tf_op jit(solution)/shard_map/all_to_all | solution.py:244
  218.5 9.3 %all-to-all-start.6 = ((f32[128,1,192]{2,1,0:T(1,128)}), f32[128,1,192]{2,1,0:T(1,128)S(1)}, u32[]{:S(2)}, u32[]{:S(2)}) async-start(f32[128,1,192]{2,1,0:T(1,128)} %reshape.1264), calls=%async_computation.6 | async-start | bytes 262144 | tf_op jit(solution)/shard_map/all_to_all | solution.py:24
  227.9 9.8 %all-to-all-done.6 = f32[128,1,192]{2,1,0:T(1,128)S(1)} async-done(((f32[128,1,192]{2,1,0:T(1,128)}), f32[128,1,192]{2,1,0:T(1,128)S(1)}, u32[]{:S(2)}, u32[]{:S(2)}) %all-to-all-start.6) | async-done | bytes 98336 | tf_op jit(solution)/shard_map/all_to_all | solution.py:24
  251.0 5.9 %reshape.1266 = f32[128,1,384]{2,1,0:T(1,128)S(1)} reshape(f32[2048,4,6]{2,1,0:T(4,128)} %bitcast.795) | data formatting | bytes 393216
  256.9 14.2 %all_to_all.167 = f32[128,1,384]{2,1,0:T(1,128)S(1)} all-to-all(f32[128,1,384]{2,1,0:T(1,128)S(1)} %reshape.1266), channel_id=1, replica_groups=mesh['row'=16,'col_0'=4,'col_1'=2] {'row','col_0','col_1'}, dimensions={0} | all-to-all | bytes 393216 | tf_op jit(solution)/shard_map/all_to_all | solution.py:24
  272.1 6.8 %reshape.1267 = f32[2048,4,6]{2,1,0:T(4,128)} reshape(f32[128,384]{1,0:T(8,128)S(1)} %reduce.31) | data formatting | bytes 393216
  278.9 5.7 %copy.318 = f32[4,6,128,16]{3,2,0,1:T(8,128)S(1)} copy(f32[4,6,128,16]{1,0,3,2:T(4,128)} %bitcast.796) | data formatting | bytes 393216 | tf_op jit(solution)/shard_map/all_to_all | solution.py:24
  306.2 8.2 %all_to_all.168 = f32[4,2,2,16,256]{4,1,3,2,0:T(2,128)S(1)} all-to-all(f32[4,2,2,16,256]{4,1,3,2,0:T(2,128)S(1)} %copy.281), channel_id=1, replica_groups=mesh['row'=16,'col_0'=4,'col_1'=2] {'col_0'}, dimensions={0} | all-to-all | bytes 524288 | tf_op jit(solution)/shard_map/all_to_all | solution.py:50
  314.5 7.9 %all_to_all.169 = f32[4,2,2,16,256]{4,0,3,2,1:T(4,128)S(1)} all-to-all(f32[4,2,2,16,256]{4,0,3,2,1:T(4,128)S(1)} %copy.282), channel_id=1, replica_groups=mesh['row'=16,'col_0'=4,'col_1'=2] {'col_1'}, dimensions={1} | all-to-all | bytes 524288 | tf_op jit(solution)/shard_map/all_to_all | solution.py:50
  342.0 8.2 %all-to-all-start.11 = ((f32[128,1,192]{2,1,0:T(1,128)}), f32[128,1,192]{2,1,0:T(1,128)S(1)}, u32[]{:S(2)}, u32[]{:S(2)}) async-start(f32[128,1,192]{2,1,0:T(1,128)} %reshape.1268), calls=%async_computation.11 | async-start | bytes 262144 | tf_op jit(solution)/shard_map/all_to_all | solution.py:24
  350.9 9.1 %all-to-all-done.11 = f32[128,1,192]{2,1,0:T(1,128)S(1)} async-done(((f32[128,1,192]{2,1,0:T(1,128)}), f32[128,1,192]{2,1,0:T(1,128)S(1)}, u32[]{:S(2)}, u32[]{:S(2)}) %all-to-all-start.11) | async-done | bytes 98336 | tf_op jit(solution)/shard_map/all_to_all | solution.py:24
  381.2 9.7 %reshape_squeeze.7 = f32[64,2,128,2]{3,2,1,0:T(8,128)} reshape(f32[1,8,16,256]{3,2,0,1:T(8,128)S(1)} %copy-done.19) | data formatting | bytes 262144 | tf_op jit(solution)/shard_map/reshape;squeeze | solution.py:88
  426.8 9.7 %reshape_squeeze.6 = f32[64,2,128,2]{3,2,1,0:T(8,128)} reshape(f32[1,8,16,256]{3,2,0,1:T(8,128)S(1)} %copy-done.18) | data formatting | bytes 262144 | tf_op jit(solution)/shard_map/reshape;squeeze | solution.py:88
  451.6 9.7 %reshape.1233 = f32[64,2,128,2]{3,2,1,0:T(8,128)} reshape(f32[128,256]{1,0:T(8,128)S(1)} %get-tuple-element.32) | data formatting | bytes 262144 | tf_op jit(solution)/shard_map/reshape | solution.py:88
  (376 shorter events, 273.2 us)
Async XLA Ops:
  3.6 15.9 %all-to-all-start = ((f32[2,128,256]{2,0,1:T(2,128)}), f32[2,128,256]{2,0,1:T(2,128)S(1)}, u32[]{:S(2)}, u32[]{:S(2)}) async-start(f32[2,128,256]{2,0,1:T(2,128)} %pad_maximum_fusion.28), calls=%async_computation | async-start | bytes 524288 | tf_op jit(solution)/shard_map/all_to_all | solution.py:244
  28.3 17.2 %all-to-all-start.1 = ((f32[128,1,384]{2,1,0:T(1,128)}), f32[128,1,384]{2,1,0:T(1,128)S(1)}, u32[]{:S(2)}, u32[]{:S(2)}) async-start(f32[128,1,384]{2,1,0:T(1,128)} %reshape.1260), calls=%async_computation.1 | async-start | bytes 393216 | tf_op jit(solution)/shard_map/all_to_all | solution.py:24
  82.2 19.5 %all-to-all-start.2 = ((f32[128,1,1344]{2,1,0:T(1,128)}), f32[128,1,1344]{2,1,0:T(1,128)S(1)}, u32[]{:S(2)}, u32[]{:S(2)}) async-start(f32[128,1,1344]{2,1,0:T(1,128)} %reshape.1262), calls=%async_computation.2 | async-start | bytes 1441792 | tf_op jit(solution)/shard_map/all_to_all | solution.py:24
  201.9 10.5 %all-to-all-start.5 = ((f32[1,128,256]{2,0,1:T(1,128)}), f32[1,128,256]{2,0,1:T(1,128)S(1)}, u32[]{:S(2)}, u32[]{:S(2)}) async-start(f32[1,128,256]{2,0,1:T(1,128)} %broadcast_in_dim.16), calls=%async_computation.5 | async-start | bytes 262144 | tf_op jit(solution)/shard_map/all_to_all | solution.py:244
  218.5 19.1 %all-to-all-start.6 = ((f32[128,1,192]{2,1,0:T(1,128)}), f32[128,1,192]{2,1,0:T(1,128)S(1)}, u32[]{:S(2)}, u32[]{:S(2)}) async-start(f32[128,1,192]{2,1,0:T(1,128)} %reshape.1264), calls=%async_computation.6 | async-start | bytes 262144 | tf_op jit(solution)/shard_map/all_to_all | solution.py:24
  306.0 17.2 %copy-start.8 = (f32[128,256]{1,0:T(8,128)S(1)}, f32[128,256]{1,0:T(8,128)}, u32[]{:S(2)}) copy-start(f32[128,256]{1,0:T(8,128)} %param.3) | copy-start | bytes 393220
  306.0 17.2 %copy-start.16 = (f32[1,8,16,256]{3,2,0,1:T(8,128)S(1)}, f32[1,8,16,256]{3,2,0,1:T(8,128)}, u32[]{:S(2)}) copy-start(f32[1,8,16,256]{3,2,0,1:T(8,128)} %get-tuple-element.57) | copy-start | bytes 393220
  306.2 21.2 %copy-start = (f32[3,16,64,128]{3,2,1,0:T(8,128)S(1)}, f32[3,16,64,128]{3,2,1,0:T(8,128)}, u32[]{:S(2)}) copy-start(f32[3,16,64,128]{3,2,1,0:T(8,128)} %param.5) | copy-start | bytes 4718596
  324.0 10.4 %all-to-all-start.10 = ((f32[1,128,256]{2,0,1:T(1,128)}), f32[1,128,256]{2,0,1:T(1,128)S(1)}, u32[]{:S(2)}, u32[]{:S(2)}) async-start(f32[1,128,256]{2,0,1:T(1,128)} %copy.284), calls=%async_computation.10 | async-start | bytes 262144 | tf_op jit(solution)/shard_map/all_to_all | solution.py:244
  342.0 17.9 %all-to-all-start.11 = ((f32[128,1,192]{2,1,0:T(1,128)}), f32[128,1,192]{2,1,0:T(1,128)S(1)}, u32[]{:S(2)}, u32[]{:S(2)}) async-start(f32[128,1,192]{2,1,0:T(1,128)} %reshape.1268), calls=%async_computation.11 | async-start | bytes 262144 | tf_op jit(solution)/shard_map/all_to_all | solution.py:24
  376.6 18.9 %all-to-all-start.12 = ((f32[128,1,192]{2,1,0:T(1,128)}), f32[128,1,192]{2,1,0:T(1,128)S(1)}, u32[]{:S(2)}, u32[]{:S(2)}) async-start(f32[128,1,192]{2,1,0:T(1,128)} %reshape.1270), calls=%async_computation.12 | async-start | bytes 262144 | tf_op jit(solution)/shard_map/all_to_all | solution.py:24
  421.5 19.7 %all-to-all-start.13 = ((f32[4,2,1,16,256]{4,1,3,2,0:T(2,128)}), f32[4,2,1,16,256]{4,1,3,2,0:T(2,128)S(1)}, u32[]{:S(2)}, u32[]{:S(2)}) async-start(f32[4,2,1,16,256]{4,1,3,2,0:T(2,128)} %copy.302), calls=%async_computation.13 | async-start | bytes 262144 | tf_op jit(solution)/shard_map/all_to_all | solution.py:50
  436.5 14.3 %copy-start.12 = (f32[1,8,16,256]{3,2,0,1:T(8,128)S(1)}, f32[1,8,16,256]{3,2,0,1:T(8,128)}, u32[]{:S(2)}) copy-start(f32[1,8,16,256]{3,2,0,1:T(8,128)} %copy-done.11) | copy-start | bytes 393220
  436.5 14.3 %copy-start.13 = (f32[1,8,16,256]{3,2,0,1:T(8,128)S(1)}, f32[1,8,16,256]{3,2,0,1:T(8,128)}, u32[]{:S(2)}) copy-start(f32[1,8,16,256]{3,2,0,1:T(8,128)} %get-tuple-element.61) | copy-start | bytes 393220
  436.5 14.3 %copy-start.15 = (f32[1,8,16,256]{3,2,0,1:T(8,128)S(1)}, f32[1,8,16,256]{3,2,0,1:T(8,128)}, u32[]{:S(2)}) copy-start(f32[1,8,16,256]{3,2,0,1:T(8,128)} %copy-done.14) | copy-start | bytes 393220
  436.5 14.3 %copy-start.17 = (f32[1,8,16,256]{3,2,0,1:T(8,128)S(1)}, f32[1,8,16,256]{3,2,0,1:T(8,128)}, u32[]{:S(2)}) copy-start(f32[1,8,16,256]{3,2,0,1:T(8,128)} %get-tuple-element.57) | copy-start | bytes 393220
  436.5 14.3 %copy-start.20 = (f32[1,8,16,256]{3,2,0,1:T(8,128)S(1)}, f32[1,8,16,256]{3,2,0,1:T(8,128)}, u32[]{:S(2)}) copy-start(f32[1,8,16,256]{3,2,0,1:T(8,128)} %get-tuple-element.69) | copy-start | bytes 393220
  436.6 14.3 %copy-start.21 = (f32[1,8,16,256]{3,2,0,1:T(8,128)S(1)}, f32[1,8,16,256]{3,2,0,1:T(8,128)}, u32[]{:S(2)}) copy-start(f32[1,8,16,256]{3,2,0,1:T(8,128)} %get-tuple-element.56) | copy-start | bytes 393220
  436.6 14.3 %copy-start.22 = (f32[1,8,16,256]{3,2,0,1:T(8,128)S(1)}, f32[1,8,16,256]{3,2,0,1:T(8,128)}, u32[]{:S(2)}) copy-start(f32[1,8,16,256]{3,2,0,1:T(8,128)} %get-tuple-element.60) | copy-start | bytes 393220
  441.9 8.8 %all-to-all-start.14 = ((f32[4,2,1,16,256]{4,0,3,2,1:T(4,128)}), f32[4,2,1,16,256]{4,0,3,2,1:T(4,128)S(1)}, u32[]{:S(2)}, u32[]{:S(2)}) async-start(f32[4,2,1,16,256]{4,0,3,2,1:T(4,128)} %copy.303), calls=%async_computation.14 | async-start | bytes 262144 | tf_op jit(solution)/shard_map/all_to_all | solution.py:50
  470.3 9.9 %collective-permute-start.2 = (f32[49,64,1]{1,2,0:T(1,128)S(1)}, f32[49,64,1]{1,2,0:T(1,128)S(1)}, u32[]{:S(2)}, u32[]{:S(2)}) collective-permute-start(f32[49,64,1]{1,2,0:T(1,128)S(1)} %copy.305), channel_id=1, source_target_pairs={{1,0},{2,1},{3,2},{4,3},{5,4},{6,5},{7,6},{0,7},{9,8},{10,9},{11,1... | collective-permute-start | bytes 37640 | tf_op jit(solution)/shard_map/ppermute | solution.py:68
  473.8 9.7 %collective-permute-start.3 = (f32[49,64,1]{1,2,0:T(1,128)}, f32[49,64,1]{1,2,0:T(1,128)}, u32[]{:S(2)}, u32[]{:S(2)}) collective-permute-start(f32[49,64,1]{1,2,0:T(1,128)} %copy.307), channel_id=1, source_target_pairs={{0,1},{1,2},{2,3},{3,4},{4,5},{5,6},{6,7},{7,0},{8,9},{9,10},{10,1... | collective-permute-start | bytes 37640 | tf_op jit(solution)/shard_map/ppermute | solution.py:67
  474.4 13.2 %collective-permute-start = (f32[49,1,128]{2,1,0:T(1,128)}, f32[49,1,128]{2,1,0:T(1,128)}, u32[]{:S(2)}, u32[]{:S(2)}) collective-permute-start(f32[49,1,128]{2,1,0:T(1,128)} %get-tuple-element.39), channel_id=1, source_target_pairs={{0,8},{8,16},{16,24},{24,32},{32,40},{40,48},{48,56},{56,64},{64,7... | collective-permute-start | bytes 75272 | tf_op jit(solution)/shard_map/ppermute | solution.py:67
  478.2 9.4 %collective-permute-start.1 = (f32[49,1,128]{2,1,0:T(1,128)}, f32[49,1,128]{2,1,0:T(1,128)}, u32[]{:S(2)}, u32[]{:S(2)}) collective-permute-start(f32[49,1,128]{2,1,0:T(1,128)} %get-tuple-element.40), channel_id=1, source_target_pairs={{8,0},{16,8},{24,16},{32,24},{40,32},{48,40},{56,48},{64,56},{72,6... | collective-permute-start | bytes 75272 | tf_op jit(solution)/shard_map/ppermute | solution.py:68
  (22 other events, 71.8 us)
where the time goes:
time: 507 us; the launch traced here: 497 us
  local copies, waits for them, and re-layouts  194 us (38%)
  waiting for transfers between devices  66.7 us (13%)
  starting transfers between devices  65.1 us (13%)
  matrix products  60.1 us (12%)
  blocking collectives  58.6 us (12%)
  other arithmetic  48.6 us (10%)
    dot_general x84, matrix products, product(): return jnp.einsum(form, left, right, precision=lax.Precision.HIGHEST)  60.1 us
    all_to_all x4, blocking collectives, exchange_in_order(): lax.all_to_all(pieces, axes[k], split_axis=k, concat_axis=k, tiled=True)  44.4 us
    unnamed x88, local copies, waits for them, and re-layouts  44 us
    all_to_all x5, waiting for transfers between devices, in_one_piece(): lax.all_to_all(both, axis, split_axis=split_dim, concat_axis=concat_dim,...  43.4 us
    all_to_all x5, starting transfers between devices, in_one_piece(): lax.all_to_all(both, axis, split_axis=split_dim, concat_axis=concat_dim,...  34.1 us
    all_to_all x4, local copies, waits for them, and re-layouts, in_one_piece(): lax.all_to_all(both, axis, split_axis=split_dim, concat_axis=concat_dim,...  19.9 us
    another operation x2, local copies, waits for them, and re-layouts, coarsen(): return source.reshape(rows_out, COARSE, cols_out, COARSE).mean(axis=(1, 3))  19.5 us
    all_to_all x3, waiting for transfers between devices, forward(): lax.all_to_all(stacked, COL, split_axis=1, concat_axis=2, tiled=True)  19.2 us
  transfers between devices with their start and end apart: 14, of which 8 were waited for; matrix products, arithmetic and copies ran while one was open for 9% of the time, Pallas kernels for 0%

commit v1 on v0

v1 whole, which is shorter than its diff:
```python
import functools

import jax
import jax.numpy as jnp
import numpy as np
from jax import lax
from jax.experimental import pallas as pl
from jax.experimental.pallas import tpu as pltpu
from jax.sharding import PartitionSpec as P

N = 2048
KEPT = N // 3
ROWS = 16
COLS = 8
DEVS = ROWS * COLS
LINES = 16
OWNERS = 86
OWN_PAD = 88
LANES = 128
LZ = 16
GRAVITY = 1.0
SURFACE_STEP = 0.05
FLOW_STEP = 0.5
VISCOSITY = 0.2
DECAY_RATE = 0.05
MESH = pl.DeviceIdType.MESH
F32 = jnp.float32
BF16 = jnp.bfloat16
VMEM = pltpu.VMEM


def block_complex(c, s):
    return np.block([[c, -s], [s, c]])


def split_table(t):
    hi = t.astype(np.float32).astype(jnp.bfloat16)
    lo = (t - hi.astype(np.float64)).astype(np.float32).astype(jnp.bfloat16)
    return hi, lo


@functools.cache
def tables():
    def wave(a, b, n):
        ang = 2.0 * np.pi * ((a[:, None] * b[None, :]) % n) / n
        return np.cos(ang), np.sin(ang)

    r8, r16, r128, r256 = (np.arange(k) for k in (8, 16, 128, 256))
    own = np.arange(OWN_PAD)
    eye16, eye8 = np.eye(16), np.eye(8)
    c8, s8 = wave(r8, r8, 8)
    c16, s16 = wave(r16, r16, 16)
    x_first = np.concatenate([np.kron(c8, eye16), np.kron(-s8, eye16)], axis=1)
    x_last = np.concatenate([np.kron(c8, eye16), np.kron(-s8, eye16)], axis=0)
    cp, sp = wave(own, r256, 256)
    x_second = block_complex(cp, -sp)
    x_third = block_complex(cp.T, sp.T)
    c1, s1 = wave(r128, r128, 128)
    y_first = block_complex(c1, -s1)
    y_last = block_complex(c1, s1)
    y_second = block_complex(np.kron(eye8, c16), np.kron(eye8, s16))
    y_third = block_complex(np.kron(eye8, c16), np.kron(eye8, -s16))
    ct, st = wave(r256, r8, N)
    x_twist = np.stack([np.repeat(ct, 16, axis=1), np.repeat(st, 16, axis=1)])
    ct, st = wave(r128, r16, N)
    y_twist = np.stack([np.tile(ct, (1, 8)), np.tile(st, (1, 8))])
    pairs = np.kron(np.eye(128), np.ones((2, 1))) * 0.25
    mats = [x_first, x_second, x_third, x_last, y_first, y_second, y_third, y_last]
    out = []
    for m in mats:
        out.extend(split_table(m))
    out.append(pairs.astype(np.float32).astype(jnp.bfloat16))
    out.append(x_twist.astype(np.float32))
    out.append(y_twist.astype(np.float32))
    return tuple(out)


def split(a):
    hi = a.astype(BF16)
    return hi, (a - hi.astype(F32)).astype(BF16)


def dot(a, b):
    return lax.dot_general(a, b, (((1,), (0,)), ((), ())), preferred_element_type=F32)


def left_table(table, data):
    th, tl = table
    dh, dl = split(data)
    return dot(th, dh) + dot(th, dl) + dot(tl, dh)


def right_table(data, table):
    th, tl = table
    dh, dl = split(data)
    return dot(dh, th) + dot(dl, th) + dot(dh, tl)


def x_forward(phys, first, second, twist):
    z = right_table(phys, first)
    zr, zi = z[:, :LANES], z[:, LANES:]
    c, s = twist
    t = jnp.concatenate([zr * c + zi * s, zi * c - zr * s], axis=0)
    out = left_table(second, t)
    return out[:OWN_PAD], out[OWN_PAD:]


def x_inverse(re, im, third, last, twist):
    u = left_table(third, jnp.concatenate([re, im], axis=0))
    ur, ui = u[:256], u[256:]
    c, s = twist
    t = jnp.concatenate([ur * c - ui * s, ur * s + ui * c], axis=1)
    return right_table(t, last)


def y_forward(re, im, first, second, twist):
    t = left_table(first, jnp.concatenate([re, im], axis=0))
    tr, ti = t[:LANES], t[LANES:]
    c, s = twist
    z = right_table(jnp.concatenate([tr * c + ti * s, ti * c - tr * s], axis=1), second)
    return z[:, :LANES], z[:, LANES:]


def y_inverse(re, im, third, last, twist):
    u = right_table(jnp.concatenate([re, im], axis=1), third)
    ur, ui = u[:, :LANES], u[:, LANES:]
    c, s = twist
    out = left_table(last, jnp.concatenate([ur * c - ui * s, ur * s + ui * c], axis=0))
    return out[:LANES], out[LANES:]


def wave_grids(p):
    lane = lax.broadcasted_iota(jnp.int32, (LANES, LANES), 1)
    q1 = lax.broadcasted_iota(jnp.int32, (LANES, LANES), 0)
    kx_index = lane // 16 + 8 * p
    ky_index = q1 + 128 * (lane % 16)
    ky_signed = jnp.where(ky_index < N // 2, ky_index, ky_index - N)
    unit = np.float32(2.0 * np.pi / N)
    kx = unit * kx_index.astype(F32)
    ky = unit * ky_signed.astype(F32)
    kept = (jnp.abs(ky_signed) <= KEPT) & (kx_index <= KEPT)
    fold = jnp.where(kx_index == 0, 1.0, 2.0) / float(N * N)
    weight = jnp.where(kept, fold, 0.0).astype(F32)
    return kx, ky, jnp.sqrt(kx * kx + ky * ky), weight


def owner_place(p):
    late = (p >= 64).astype(jnp.int32)
    chip = p + late * (2 * p - 192)
    return 2 * (chip // COLS) + late, chip % COLS


def get(buf, j, count):
    return buf[:count, j, :]


def put(buf, j, value):
    buf[: value.shape[0], j, :] = value


def surface_kernel(*refs):
    phi_ref, eta_ref, vel_ref = refs[:3]
    n_tab = 19
    tab = refs[3 : 3 + n_tab]
    outs = refs[3 + n_tab : 3 + n_tab + 10]
    (height_out, pot_out, su_out, sv_out, lx_out, press_out, low_y, high_y, low_x, high_x) = outs
    (
        lines,
        fields,
        send1,
        recv1,
        send2,
        recv2,
        send2b,
        recv2b,
        send3,
        recv3,
        send4,
        recv4,
        send5,
        recv5,
        send6,
        recv6,
        spec,
        turned,
        out_t,
        coarse_t,
        vel,
        pack_y,
        pack_x,
        vel_sem,
        send_sems,
        recv_sems,
        out_sems,
        halo_sems,
    ) = refs[3 + n_tab + 10 :]
    row, col = lax.axis_index("row"), lax.axis_index("col")
    me = row * COLS + col
    chip = (row // 2) * COLS + col
    core = row % 2
    is_owner = (core == 0) | (chip % 3 == 0)
    my_p = jnp.where(core == 0, chip, 64 + chip // 3)

    def tables_at(k):
        return tab[2 * k][...], tab[2 * k + 1][...]

    pairs_ref, x_twist_ref, y_twist_ref = tab[16:19]

    def remote(src, dst, send_sem, recv_sem, place):
        return pltpu.make_async_remote_copy(
            src_ref=src,
            dst_ref=dst,
            send_sem=send_sem,
            recv_sem=recv_sem,
            device_id=place,
            device_id_type=MESH,
        )

    def wait_bytes(ref, sem):
        pltpu.make_async_copy(ref, ref, sem).wait()

    vel_copy = pltpu.make_async_copy(vel_ref, vel, vel_sem)
    vel_copy.start()

    barrier = pltpu.get_barrier_semaphore()

    def greet(i, _):
        other = lax.rem(me + i, DEVS)
        pl.semaphore_signal(barrier, inc=1, device_id=(other // COLS, other % COLS), device_id_type=MESH)
        return 0

    lax.fori_loop(1, DEVS, greet, 0)
    for buf in (recv2, recv2b, recv4, recv6):
        buf[OWNERS:OWN_PAD] = jnp.zeros((OWN_PAD - OWNERS,) + buf.shape[1:], F32)
    pl.semaphore_wait(barrier, DEVS - 1)

    for f, ref in enumerate((phi_ref, eta_ref)):
        for i in range(1, COLS):
            to = lax.rem(col + i, COLS)
            remote(
                ref.at[pl.ds(to * LINES, LINES), :],
                lines.at[f, col],
                send_sems.at[f],
                recv_sems.at[f],
                (row, to),
            ).start()
        pltpu.make_async_copy(
            ref.at[pl.ds(col * LINES, LINES), :], lines.at[f, col], recv_sems.at[f]
        ).start()

    def to_owners(send, recv, k):
        def step(i, _):
            p = lax.rem(me + i, OWNERS)
            r, c = owner_place(p)

            @pl.when(r * COLS + c != me)
            def _():
                remote(send.at[p], recv.at[me], send_sems.at[k], recv_sems.at[k], (r, c)).start()

            @pl.when(r * COLS + c == me)
            def _():
                pltpu.make_async_copy(send.at[p], recv.at[me], recv_sems.at[k]).start()

            return 0

        lax.fori_loop(0, OWNERS, step, 0)

    def to_lines(send, recv, k):
        def step(i, _):
            other = lax.rem(me + i, DEVS)
            remote(
                send.at[other],
                recv.at[my_p],
                send_sems.at[k],
                recv_sems.at[k],
                (other // COLS, other % COLS),
            ).start()
            return 0

        lax.fori_loop(1, DEVS, step, 0)
        pltpu.make_async_copy(send.at[me], recv.at[my_p], recv_sems.at[k]).start()

    def forward_x(f, send, j):
        re, im = x_forward(fields[f], tables_at(0), tables_at(1), (x_twist_ref[0], x_twist_ref[1]))
        put(send, 2 * j, re)
        put(send, 2 * j + 1, im)

    def inverse_x(recv, j):
        re, im = get(recv, 2 * j, OWN_PAD), get(recv, 2 * j + 1, OWN_PAD)
        return x_inverse(re, im, tables_at(2), tables_at(3), (x_twist_ref[0], x_twist_ref[1]))

    y_twist = lambda: (y_twist_ref[0], y_twist_ref[1])

    def forward_y(recv, j):
        re, im = get(recv, 2 * j, DEVS), get(recv, 2 * j + 1, DEVS)
        return y_forward(re, im, tables_at(4), tables_at(5), y_twist())

    def inverse_y(re, im, send, j):
        re, im = y_inverse(re, im, tables_at(6), tables_at(7), y_twist())
        put(send, 2 * j, re)
        put(send, 2 * j + 1, im)

    vel_copy.wait()
    lane = lax.broadcasted_iota(jnp.int32, (64, LANES), 1)
    pack_y[0] = vel[:, 63, :]
    pack_y[1] = vel[:, 0, :]

    def pack(b, carry):
        last, first = carry
        value = vel[b]
        last = jnp.where(lane == b, pltpu.roll(value, b + 1, axis=1), last)
        first = jnp.where(lane == b, pltpu.roll(value, b, axis=1), first)
        return last, first

    zero = jnp.zeros((64, LANES), F32)
    last, first = lax.fori_loop(0, 3 * LZ, pack, (zero, zero))
    pack_x[0] = last
    pack_x[1] = first
    up_r, down_r = lax.rem(row + 1, ROWS), lax.rem(row + ROWS - 1, ROWS)
    up_c, down_c = lax.rem(col + 1, COLS), lax.rem(col + COLS - 1, COLS)
    halos = [
        remote(pack_y.at[0], low_y, halo_sems.at[0], halo_sems.at[4], (up_r, col)),
        remote(pack_y.at[1], high_y, halo_sems.at[1], halo_sems.at[5], (down_r, col)),
        remote(pack_x.at[0], low_x, halo_sems.at[2], halo_sems.at[6], (row, up_c)),
        remote(pack_x.at[1], high_x, halo_sems.at[3], halo_sems.at[7], (row, down_c)),
    ]
    for h in halos:
        h.start()

    for f in range(2):
        wait_bytes(lines.at[f], recv_sems.at[f])
        fields[f] = jnp.transpose(lines[f].reshape(LANES, 256))
        forward_x(f, send1, f)
    to_owners(send1, recv1, 2)

    @pl.when(is_owner)
    def _():
        wait_bytes(recv1, recv_sems.at[2])
        kx, ky, mag, weight = wave_grids(my_p)
        for f in range(2):
            re, im = forward_y(recv1, f)
            spec[2 * f] = re * weight
            spec[2 * f + 1] = im * weight
        inverse_y(spec[0] * mag, spec[1] * mag, send2, 0)
        to_lines(send2, recv2, 3)
        turned[0] = mag * mag * spec[0]
        turned[1] = mag * mag * spec[1]
        turned[2] = mag * mag * mag * spec[0]
        turned[3] = mag * mag * mag * spec[1]
        for f in range(2):
            turned[4 + 4 * f] = -kx * spec[2 * f + 1]
            turned[5 + 4 * f] = kx * spec[2 * f]
            turned[6 + 4 * f] = -ky * spec[2 * f + 1]
            turned[7 + 4 * f] = ky * spec[2 * f]
        for j in range(6):
            inverse_y(turned[2 * j], turned[2 * j + 1], send2b, j)
        to_lines(send2b, recv2b, 4)

    wait_bytes(recv2.at[:OWNERS], recv_sems.at[3])
    vert = inverse_x(recv2, 0)
    fields[2] = vert
    fields[0] = -fields[1] * vert
    forward_x(0, send3, 0)
    to_owners(send3, recv3, 5)

    @pl.when(is_owner)
    def _():
        wait_bytes(recv3, recv_sems.at[5])
        kx, ky, mag, weight = wave_grids(my_p)
        re, im = forward_y(recv3, 0)
        first_factor = weight * mag
        second_factor = first_factor * mag
        inverse_y(re * first_factor, im * first_factor, send4, 0)
        inverse_y(re * second_factor, im * second_factor, send4, 1)
        to_lines(send4, recv4, 6)

    wait_bytes(recv2b.at[:OWNERS], recv_sems.at[4])
    for j in range(6):
        fields[3 + j] = inverse_x(recv2b, j)

    wait_bytes(recv4.at[:OWNERS], recv_sems.at[6])
    vert_two = inverse_x(recv4, 0)
    eta = fields[1]
    fields[0] = -eta * vert_two - 0.5 * eta * eta * fields[3]
    forward_x(0, send5, 0)
    to_owners(send5, recv5, 7)

    @pl.when(is_owner)
    def _():
        wait_bytes(recv5, recv_sems.at[7])
        kx, ky, mag, weight = wave_grids(my_p)
        re, im = forward_y(recv5, 0)
        factor = weight * mag
        inverse_y(re * factor, im * factor, send6, 0)
        to_lines(send6, recv6, 8)

    curve_two = inverse_x(recv4, 1)
    eta = fields[1]
    fields[2] = fields[2] + vert_two + eta * (fields[3] + curve_two) + 0.5 * eta * eta * fields[4]
    pot_dx, pot_dy, height_dx, height_dy = (fields[5 + j] for j in range(4))
    fields[7] = 1.0 + (height_dx * height_dx + height_dy * height_dy)
    fields[3] = -(height_dx * pot_dx + height_dy * pot_dy)
    fields[4] = -GRAVITY * eta - 0.5 * (pot_dx * pot_dx + pot_dy * pot_dy)

    def coarsen(j):
        hi, lo = split(out_t[j])
        spec[0] = dot(hi, pairs_ref[...]) + dot(lo, pairs_ref[...])
        return spec[0, pl.ds(0, 64, stride=2), :] + spec[0, pl.ds(1, 64, stride=2), :]

    out_t[2] = jnp.transpose(pot_dx)
    out_t[3] = jnp.transpose(pot_dy)
    coarse_t[0] = coarsen(2)
    coarse_t[1] = coarsen(3)

    wait_bytes(recv6.at[:OWNERS], recv_sems.at[8])
    vertical = fields[2] + inverse_x(recv6, 0)
    scaled = fields[7] * vertical
    height_rate = fields[3] + scaled
    out_t[0] = jnp.transpose(height_rate)
    out_t[1] = jnp.transpose(fields[4] + 0.5 * scaled * vertical)
    out_t[2] = jnp.transpose(GRAVITY * (fields[1] + SURFACE_STEP * height_rate))
    pressure = coarsen(2)
    coarse_t[2] = pressure
    lane64 = lax.broadcasted_iota(jnp.int32, (64, LANES), 1)
    east = pltpu.roll(pressure, LANES - 1, axis=1)
    east = jnp.where(lane64 == LANES - 1, pltpu.roll(east, 56, axis=0), east)
    west = pltpu.roll(pressure, 1, axis=1)
    west = jnp.where(lane64 == 0, pltpu.roll(west, 8, axis=0), west)
    coarse_t[3] = 0.5 * (east - west)

    def pieces(to):
        fine = pl.ds(to * LINES, LINES)
        few = pl.ds(to * 8, 8)
        mine = pl.ds(col * LINES, LINES)
        my_few = pl.ds(col * 8, 8)
        return [
            (out_t.at[0, fine, :], height_out.at[mine, :]),
            (out_t.at[1, fine, :], pot_out.at[mine, :]),
            (coarse_t.at[0, few, :], su_out.at[my_few, :]),
            (coarse_t.at[1, few, :], sv_out.at[my_few, :]),
            (coarse_t.at[3, few, :], lx_out.at[my_few, :]),
            (coarse_t.at[2, few, :], press_out.at[pl.ds(col * 8 + 8, 8), :]),
        ]

    for i in range(1, COLS):
        to = lax.rem(col + i, COLS)
        for k, (src, dst) in enumerate(pieces(to)):
            remote(src, dst, out_sems.at[k], out_sems.at[6 + k], (row, to)).start()
    for k, (src, dst) in enumerate(pieces(col)):
        pltpu.make_async_copy(src, dst, out_sems.at[6 + k]).start()

    @pl.when(col == COLS - 1)
    def _():
        for to in range(COLS):
            remote(
                coarse_t.at[2, pl.ds(to * 8, 8), :],
                press_out.at[pl.ds(0, 8), :],
                out_sems.at[12],
                out_sems.at[11],
                (up_r, to),
            ).start()

    @pl.when(col == 0)
    def _():
        for to in range(COLS):
            remote(
                coarse_t.at[2, pl.ds(to * 8, 8), :],
                press_out.at[pl.ds(72, 8), :],
                out_sems.at[12],
                out_sems.at[11],
                (down_r, to),
            ).start()

    for k, ref in enumerate((height_out, pot_out, su_out, sv_out, lx_out, press_out)):
        wait_bytes(ref, out_sems.at[6 + k])

    for h in halos:
        h.wait()
    for f in range(2):
        wait_bytes(lines.at[f, :7], send_sems.at[f])
    for k in range(2):
        wait_bytes(out_t.at[k, :112, :], out_sems.at[k])
    for k in range(4):
        wait_bytes(coarse_t.at[k, :56, :], out_sems.at[2 + k])

    @pl.when((col == 0) | (col == COLS - 1))
    def _():
        wait_bytes(coarse_t.at[2], out_sems.at[12])

    @pl.when(is_owner)
    def _():
        for buf, k in ((send1, 2), (send3, 5), (send5, 7)):
            wait_bytes(buf.at[: OWNERS - 1], send_sems.at[k])
        for buf, k in ((send2, 3), (send2b, 4), (send4, 6), (send6, 8)):
            wait_bytes(buf.at[: DEVS - 1], send_sems.at[k])

    @pl.when(jnp.logical_not(is_owner))
    def _():
        for buf, k in ((send1, 2), (send3, 5), (send5, 7)):
            wait_bytes(buf.at[:OWNERS], send_sems.at[k])


def flow_kernel(vel, su_ref, sv_ref, lx_ref, press, low_y, high_y, low_x, high_x, out):
    shape = (64, LANES)
    lane = lax.broadcasted_iota(jnp.int32, shape, 1)
    line = lax.broadcasted_iota(jnp.int32, shape, 0)
    su, sv = su_ref[...], sv_ref[...]
    load_x = lx_ref[...]
    load_y = 0.5 * (press[9:73, :] - press[7:71, :])
    from_low, from_high = low_x[...], high_x[...]

    def derivs(q, l, top):
        b = q * LZ + l
        mid = vel[b]
        above = jnp.where(l == 0, top, vel[q * LZ + jnp.maximum(l - 1, 0)])
        below = vel[q * LZ + jnp.minimum(l + 1, LZ - 1)]
        east = jnp.where(
            lane == LANES - 1,
            pltpu.roll(from_high, LANES - 1 - b, axis=1),
            pltpu.roll(mid, LANES - 1, axis=1),
        )
        west = jnp.where(
            lane == 0,
            pltpu.roll(from_low, lax.rem(LANES - b, LANES), axis=1),
            pltpu.roll(mid, 1, axis=1),
        )
        north = jnp.where(line == 63, high_y[pl.ds(b, 1), :], pltpu.roll(mid, 63, axis=0))
        south = jnp.where(line == 0, low_y[pl.ds(b, 1), :], pltpu.roll(mid, 1, axis=0))
        lap = east + west + north + south + above + below - 6.0 * mid
        return mid, 0.5 * (east - west), 0.5 * (north - south), 0.5 * (above - below), lap

    def level(l, _):
        depth = jnp.full(shape, l, jnp.int32).astype(F32) + 0.5
        load_decay = jnp.exp(-DECAY_RATE * depth)
        drift_decay = jnp.exp(-2.0 * DECAY_RATE * depth)
        u, u_dx, u_dy, u_dz, u_lap = derivs(0, l, su)
        v, v_dx, v_dy, v_dz, v_lap = derivs(1, l, sv)
        w, w_dx, w_dy, w_dz, w_lap = derivs(2, l, jnp.zeros(shape, F32))
        vort_x = w_dy - v_dz
        vort_y = u_dz - w_dx
        vort_z = v_dx - u_dy
        drift_u = su * drift_decay
        drift_v = sv * drift_decay

        def advance(mid, dx, dy, dz, lap, force):
            carried = u * dx + v * dy + w * dz
            return mid + FLOW_STEP * (-carried + VISCOSITY * lap + force)

        out[l] = advance(u, u_dx, u_dy, u_dz, u_lap, drift_v * vort_z - load_x * load_decay)
        out[LZ + l] = advance(v, v_dx, v_dy, v_dz, v_lap, -drift_u * vort_z - load_y * load_decay)
        out[2 * LZ + l] = advance(w, w_dx, w_dy, w_dz, w_lap, drift_u * vort_y - drift_v * vort_x)
        return 0

    lax.fori_loop(0, LZ, level, 0)


def local(surface_height, surface_potential, velocity):
    flow = velocity.reshape(3 * LZ, 64, LANES)
    tabs = [jnp.asarray(t) for t in tables()]
    in_vmem = pl.BlockSpec(memory_space=VMEM)

    def shape(*dims):
        return jax.ShapeDtypeStruct(dims, F32)

    def buf(*dims):
        return VMEM(dims, F32)

    messages = []
    for kind, count in (("o", 4), ("l", 2), ("l", 12), ("o", 2), ("l", 4), ("o", 2), ("l", 2)):
        if kind == "o":
            messages += [buf(OWN_PAD, count, LANES), buf(DEVS, count, LANES)]
        else:
            messages += [buf(DEVS, count, LANES), buf(OWN_PAD, count, LANES)]
    outs = pl.pallas_call(
        surface_kernel,
        name="surface",
        out_shape=[
            shape(128, 256),
            shape(128, 256),
            shape(64, LANES),
            shape(64, LANES),
            shape(64, LANES),
            shape(80, LANES),
            shape(48, LANES),
            shape(48, LANES),
            shape(64, LANES),
            shape(64, LANES),
        ],
        in_specs=[in_vmem, in_vmem, pl.BlockSpec(memory_space=pl.ANY)] + [in_vmem] * len(tabs),
        out_specs=[in_vmem] * 10,
        scratch_shapes=[buf(2, COLS, LINES, 256), buf(9, 256, LANES)]
        + messages
        + [
            buf(4, LANES, LANES),
            buf(12, LANES, LANES),
            buf(4, LANES, 256),
            buf(4, 64, LANES),
            buf(48, 64, LANES),
            buf(2, 48, LANES),
            buf(2, 64, LANES),
            pltpu.SemaphoreType.DMA,
            pltpu.SemaphoreType.DMA((9,)),
            pltpu.SemaphoreType.DMA((9,)),
            pltpu.SemaphoreType.DMA((13,)),
            pltpu.SemaphoreType.DMA((8,)),
        ],
        compiler_params=pltpu.CompilerParams(
            collective_id=0, has_side_effects=True, vmem_limit_bytes=56 * 1024 * 1024
        ),
    )(surface_potential, surface_height, flow, *tabs)
    height_rate, potential_rate = outs[:2]
    nxt = pl.pallas_call(
        flow_kernel,
        name="flow",
        out_shape=shape(3 * LZ, 64, LANES),
        in_specs=[in_vmem] * 9,
        out_specs=in_vmem,
        compiler_params=pltpu.CompilerParams(vmem_limit_bytes=32 * 1024 * 1024),
    )(flow, *outs[2:])
    return height_rate, potential_rate, nxt.reshape(velocity.shape)


def solution(mesh):
    specs = (P("row", "col"), P("row", "col"), P(None, None, "row", "col"))
    return jax.shard_map(local, mesh=mesh, in_specs=specs, out_specs=specs, check_vma=False)
```

time: 507 us -> 101 us (0.20); the launches traced: 497 us -> 100 us
  local copies, waits for them, and re-layouts: 194 us -> 7.35 us
  Pallas kernels: 0 us -> 92.1 us
  waiting for transfers between devices: 66.7 us -> 0 us
  starting transfers between devices: 65.1 us -> 0 us
  matrix products: 60.1 us -> 0 us
  blocking collectives: 58.6 us -> 0 us
  other arithmetic: 48.6 us -> 0 us
    pallas_call x0 -> x2, Pallas kernels: none -> 92.1 us  [the longest x1 87.7 us: local(): pl.pallas_call(surface_kernel, name='surface', out_shape=[shape(128, 256)...]
    all_to_all x10 -> x0, waiting for transfers between devices: 66.7 us -> none  [the longest x5 43.4 us: in_one_piece(): lax.all_to_all(both, axis, split_axis=split_dim, concat_axis=concat_dim,...]
    dot_general x84 -> x0, matrix products: 60.1 us -> none  [product(): return jnp.einsum(form, left, right, precision=lax.Precision.HIGHEST)]
    all_to_all x5 -> x0, blocking collectives: 58.6 us -> none  [the longest x4 44.4 us: exchange_in_order(): lax.all_to_all(pieces, axes[k], split_axis=k, concat_axis=k, tiled=True)]
    all_to_all x10 -> x0, starting transfers between devices: 58 us -> none  [the longest x5 34.1 us: in_one_piece(): lax.all_to_all(both, axis, split_axis=split_dim, concat_axis=concat_dim,...]
    unnamed x88 -> x24, local copies, waits for them, and re-layouts: 44 us -> 7.35 us
    reshape x32 -> x0, local copies, waits for them, and re-layouts: 33.4 us -> none  [the longest x1 9.72 us: coarsen(): return source.reshape(rows_out, COARSE, cols_out, COARSE).mean(axis=(1, 3))]
    concatenate x12 -> x0, local copies, waits for them, and re-layouts: 32.7 us -> none  [the longest x6 11.8 us: in_one_piece(): both = jnp.concatenate(arrays, axis=along)]
  transfers between devices with their start and end apart: 14 -> 0, of which waited for: 8 -> 0; matrix products, arithmetic and copies ran while one was open for 9% -> 0% of each run, Pallas kernels for 0% -> 0%
where the time goes in v1:
time: 101 us; the launch traced here: 100 us
  Pallas kernels  92.1 us (91%)
  local copies, waits for them, and re-layouts  7.35 us (7%)
    pallas_call x1, Pallas kernels, local(): pl.pallas_call(surface_kernel, name='surface', out_shape=[shape(128, 256)...  87.7 us
    unnamed x24, local copies, waits for them, and re-layouts  7.35 us
    pallas_call x1, Pallas kernels, local(): pl.pallas_call(flow_kernel, name='flow', out_shape=shape(3 * LZ, 64, LANE...  4.42 us

profile of v1, /device:TPU:1, one launch (start us, length us, event | category | flops | bytes accessed | tf_op | source)
XLA Modules:
  0.0 100.1 jit_solution(14869824384065928824)
XLA Ops:
  0.6 0.0 copy-start
  0.6 87.7 %surface.1 = (f32[128,256]{1,0:T(8,128)}, f32[128,256]{1,0:T(8,128)}, f32[64,128]{1,0:T(8,128)}, f32[64,128]{1,0:T(8,128)}, f32[64,128]{1,0:T(8,128)}, /*index=5...) custom-call(f32[128,256]{1,0:T(8,128)} %refs_0_.1, ...), custom_call_target="tpu_custom_call" | custom-call | tf_op jit(solution)/shard_map/surface/pallas_call | solution.py:574
  88.3 0.0 copy-done
  88.4 0.0 copy-start.1
  88.4 0.8 copy-done.1
  89.1 0.0 copy-start.2
  89.1 0.8 copy-done.2
  89.9 0.0 copy-start.3
  89.9 0.8 copy-done.3
  90.7 0.0 copy-start.4
  90.7 0.8 copy-done.4
  91.4 0.0 copy-start.5
  91.4 0.8 copy-done.5
  92.2 0.0 copy-start.6
  92.2 0.8 copy-done.6
  92.9 0.0 copy-start.7
  92.9 0.7 copy-done.7
  93.7 0.0 copy-start.8
  93.7 0.7 copy-done.8
  94.4 4.4 %flow.1 = f32[48,64,128]{2,1,0:T(8,128)} custom-call(f32[48,64,128]{2,1,0:T(8,128)S(1)} %bitcast.3, f32[64,128]{1,0:T(8,128)S(1)} %copy-done.2, f32[64,128]{1,0:T(8,128)S(1)} %copy-done.3, f32[64,128]{1,0:T(8,128)S(1)} %copy-done.4, f32[80,128]{1,0:T(8,128)S(1)} %copy-done.1, f32[48,128]{1,0:T(8,128)S(1)} %copy-done.7, f32[48,128]{1,0:T(8,128)S(1)} %copy-done.8, ...), custom_call_target="tpu_custom_call" | custom-call | tf_op jit(solution)/shard_map/flow/pallas_call | solution.py:612
  98.8 0.0 copy-done.10
  98.8 0.7 copy.27
  99.5 0.0 copy-done.9
  99.5 0.7 copy.28
  (2 shorter events, 0.0 us)
Async XLA Ops:
  0.6 87.7 %copy-start = (f32[3,16,64,128]{3,2,1,0:T(8,128)S(1)}, f32[3,16,64,128]{3,2,1,0:T(8,128)}, u32[]{:S(2)}) copy-start(f32[3,16,64,128]{3,2,1,0:T(8,128)} %param.24) | copy-start | bytes 4718596
  88.4 0.8 copy-start.1
  89.1 0.8 copy-start.2
  89.9 0.8 copy-start.3
  90.7 0.8 copy-start.4
  91.4 0.8 copy-start.5
  92.2 0.8 copy-start.6
  92.9 0.7 copy-start.7
  93.7 0.7 copy-start.8
  94.4 4.4 %copy-start.10 = (f32[128,256]{1,0:T(8,128)S(1)}, f32[128,256]{1,0:T(8,128)}, u32[]{:S(2)}) copy-start(f32[128,256]{1,0:T(8,128)} %get-tuple-element.26) | copy-start | bytes 393220
  94.4 5.1 %copy-start.9 = (f32[128,256]{1,0:T(8,128)S(1)}, f32[128,256]{1,0:T(8,128)}, u32[]{:S(2)}) copy-start(f32[128,256]{1,0:T(8,128)} %get-tuple-element.27) | copy-start | bytes 393220

commit v2 on v1

v2 whole, which is shorter than its diff:
```python
import functools

import jax
import jax.numpy as jnp
import numpy as np
from jax import lax
from jax.experimental import pallas as pl
from jax.experimental.pallas import tpu as pltpu
from jax.sharding import PartitionSpec as P

N = 2048
KEPT = N // 3
ROWS = 16
COLS = 8
DEVS = ROWS * COLS
LINES = 16
OWNERS = 86
OWN_PAD = 88
LANES = 128
LZ = 16
GRAVITY = 1.0
SURFACE_STEP = 0.05
FLOW_STEP = 0.5
VISCOSITY = 0.2
DECAY_RATE = 0.05
LOGICAL = pl.DeviceIdType.LOGICAL
EARLY_LEVELS = 8
F32 = jnp.float32
BF16 = jnp.bfloat16
VMEM = pltpu.VMEM


def block_complex(c, s):
    return np.block([[c, -s], [s, c]])


def split_table(t):
    hi = t.astype(np.float32).astype(jnp.bfloat16)
    lo = (t - hi.astype(np.float64)).astype(np.float32).astype(jnp.bfloat16)
    return hi, lo


@functools.cache
def tables():
    def wave(a, b, n):
        ang = 2.0 * np.pi * ((a[:, None] * b[None, :]) % n) / n
        return np.cos(ang), np.sin(ang)

    r8, r16, r128, r256 = (np.arange(k) for k in (8, 16, 128, 256))
    own = np.arange(OWN_PAD)
    eye16, eye8 = np.eye(16), np.eye(8)
    c8, s8 = wave(r8, r8, 8)
    c16, s16 = wave(r16, r16, 16)
    x_first = np.concatenate([np.kron(c8, eye16), np.kron(-s8, eye16)], axis=1)
    x_last = np.concatenate([np.kron(c8, eye16), np.kron(-s8, eye16)], axis=0)
    cp, sp = wave(own, r256, 256)
    x_second = block_complex(cp, -sp)
    x_third = block_complex(cp.T, sp.T)
    c1, s1 = wave(r128, r128, 128)
    y_first = block_complex(c1, -s1)
    y_last = block_complex(c1, s1)
    y_second = block_complex(np.kron(eye8, c16), np.kron(eye8, s16))
    y_third = block_complex(np.kron(eye8, c16), np.kron(eye8, -s16))
    ct, st = wave(r256, r8, N)
    x_twist = np.stack([np.repeat(ct, 16, axis=1), np.repeat(st, 16, axis=1)])
    ct, st = wave(r128, r16, N)
    y_twist = np.stack([np.tile(ct, (1, 8)), np.tile(st, (1, 8))])
    pairs = np.kron(np.eye(128), np.ones((2, 1))) * 0.25
    mats = [x_first, x_second, x_third, x_last, y_first, y_second, y_third, y_last]
    out = []
    for m in mats:
        out.extend(split_table(m))
    out.append(pairs.astype(np.float32).astype(jnp.bfloat16))
    out.append(x_twist.astype(np.float32))
    out.append(y_twist.astype(np.float32))
    return tuple(out)


def split(a):
    hi = a.astype(BF16)
    return hi, (a - hi.astype(F32)).astype(BF16)


def dot(a, b):
    return lax.dot_general(a, b, (((1,), (0,)), ((), ())), preferred_element_type=F32)


def left_table(table, data):
    th, tl = table
    dh, dl = split(data)
    return dot(th, dh) + dot(th, dl) + dot(tl, dh)


def right_table(data, table):
    th, tl = table
    dh, dl = split(data)
    return dot(dh, th) + dot(dl, th) + dot(dh, tl)


def x_forward(phys, first, second, twist):
    z = right_table(phys, first)
    zr, zi = z[:, :LANES], z[:, LANES:]
    c, s = twist
    t = jnp.concatenate([zr * c + zi * s, zi * c - zr * s], axis=0)
    out = left_table(second, t)
    return out[:OWN_PAD], out[OWN_PAD:]


def x_inverse(re, im, third, last, twist):
    u = left_table(third, jnp.concatenate([re, im], axis=0))
    ur, ui = u[:256], u[256:]
    c, s = twist
    t = jnp.concatenate([ur * c - ui * s, ur * s + ui * c], axis=1)
    return right_table(t, last)


def y_forward(re, im, first, second, twist):
    t = left_table(first, jnp.concatenate([re, im], axis=0))
    tr, ti = t[:LANES], t[LANES:]
    c, s = twist
    z = right_table(jnp.concatenate([tr * c + ti * s, ti * c - tr * s], axis=1), second)
    return z[:, :LANES], z[:, LANES:]


def y_inverse(re, im, third, last, twist):
    u = right_table(jnp.concatenate([re, im], axis=1), third)
    ur, ui = u[:, :LANES], u[:, LANES:]
    c, s = twist
    out = left_table(last, jnp.concatenate([ur * c - ui * s, ur * s + ui * c], axis=0))
    return out[:LANES], out[LANES:]


def wave_grids(p):
    lane = lax.broadcasted_iota(jnp.int32, (LANES, LANES), 1)
    q1 = lax.broadcasted_iota(jnp.int32, (LANES, LANES), 0)
    kx_index = lane // 16 + 8 * p
    ky_index = q1 + 128 * (lane % 16)
    ky_signed = jnp.where(ky_index < N // 2, ky_index, ky_index - N)
    unit = np.float32(2.0 * np.pi / N)
    kx = unit * kx_index.astype(F32)
    ky = unit * ky_signed.astype(F32)
    kept = (jnp.abs(ky_signed) <= KEPT) & (kx_index <= KEPT)
    fold = jnp.where(kx_index == 0, 1.0, 2.0) / float(N * N)
    weight = jnp.where(kept, fold, 0.0).astype(F32)
    return kx, ky, jnp.sqrt(kx * kx + ky * ky), weight


def get(buf, j, count):
    return buf[:count, j, :]


def put(buf, j, value):
    buf[: value.shape[0], j, :] = value


def far_first():
    hops = (0, 1, 2, 1)
    offsets = [(a, b, c) for a in range(4) for b in range(4) for c in range(4)]
    return sorted(offsets, key=lambda o: -(hops[o[0]] + hops[o[1]] + hops[o[2]]))


def surface_kernel(*refs):
    phi_ref, eta_ref, vel_ref = refs[:3]
    n_tab = 19
    tab_in = refs[3 : 3 + n_tab]
    at = 3 + n_tab
    height_out, pot_out, lx_out, press_out, base_out = refs[at : at + 5]
    at += 5
    tab = refs[at : at + n_tab]
    at += n_tab
    (
        lines,
        fields,
        send1,
        recv1,
        send1b,
        recv1b,
        send2,
        recv2,
        send2b,
        recv2b,
        send2c,
        recv2c,
        send3,
        recv3,
        send4,
        recv4,
        send4b,
        recv4b,
        send5,
        recv5,
        send6,
        recv6,
        spec,
        out_t,
        coarse_t,
        vel,
        base,
        pack_y,
        pack_x,
        low_y,
        high_y,
        low_x,
        high_x,
        su_tile,
        sv_tile,
        ids,
        own_ids,
        own_ps,
        load_sems,
        send_sems,
        recv_sems,
        out_sems,
        halo_sems,
    ) = refs[at:]
    row, col = lax.axis_index("row"), lax.axis_index("col")
    me = row * COLS + col
    is_owner = me % 3 != 2
    my_p = me - me // 3

    def remote(src, dst, send_sem, recv_sem, place):
        return pltpu.make_async_remote_copy(
            src_ref=src,
            dst_ref=dst,
            send_sem=send_sem,
            recv_sem=recv_sem,
            device_id=place,
            device_id_type=LOGICAL,
        )

    def wait_bytes(ref, sem):
        pltpu.make_async_copy(ref, ref, sem).wait()

    barrier = pltpu.get_barrier_semaphore()
    for i in range(1, COLS):
        pl.semaphore_signal(
            barrier, inc=1, device_id=row * COLS + (col + i) % COLS, device_id_type=LOGICAL
        )
    for i in range(1, ROWS):
        pl.semaphore_signal(
            barrier, inc=1, device_id=((row + i) % ROWS) * COLS + col, device_id_type=LOGICAL
        )
    vel_copy = pltpu.make_async_copy(vel_ref, vel, load_sems.at[n_tab])
    vel_copy.start()
    loads = [
        pltpu.make_async_copy(src, dst, load_sems.at[k])
        for k, (src, dst) in enumerate(zip(tab_in, tab))
    ]
    for load in loads:
        load.start()

    x_at = (col % 2) * 2 + row // 8
    y_at = (row // 2) % 4
    z_at = col // 2
    x_part = [((x_at + d) % 4) % 2 * 64 + ((x_at + d) % 4) // 2 for d in range(4)]
    y_part = [((y_at + d) % 4) * 16 for d in range(4)]
    z_part = [((z_at + d) % 4) * 2 for d in range(4)]
    core = row % 2
    cores = (8 * (1 - core), 8 * core)
    slot = jnp.int32(0)
    entry = 0
    for dx, dy, dz in far_first():
        chip = x_part[dx] + y_part[dy] + z_part[dz]
        for side in cores:
            place = chip + side
            third = place // 3
            ids[entry] = place
            own_ids[slot] = place
            own_ps[slot] = place - third
            slot = slot + (place - 3 * third < 2).astype(jnp.int32)
            entry += 1

    for buf in (recv2, recv2b, recv2c, recv4, recv4b, recv6):
        buf[OWNERS:OWN_PAD] = jnp.zeros((OWN_PAD - OWNERS,) + buf.shape[1:], F32)
    pl.semaphore_wait(barrier, COLS + ROWS - 2)

    for f, ref in enumerate((phi_ref, eta_ref)):
        for i in (4, 5, 3, 6, 2, 7, 1):
            to = (col + i) % COLS
            remote(
                ref.at[pl.ds(to * LINES, LINES), :],
                lines.at[f, col],
                send_sems.at[f],
                recv_sems.at[f],
                row * COLS + to,
            ).start()
        pltpu.make_async_copy(
            ref.at[pl.ds(col * LINES, LINES), :], lines.at[f, col], recv_sems.at[f]
        ).start()

    def to_owners(send, recv, k):
        def step(i, _):
            remote(
                send.at[own_ps[i]], recv.at[me], send_sems.at[k], recv_sems.at[k], own_ids[i]
            ).start()
            return 0

        lax.fori_loop(0, OWNERS - 1, step, 0, unroll=5)

        @pl.when(is_owner)
        def _():
            pltpu.make_async_copy(send.at[my_p], recv.at[me], recv_sems.at[k]).start()

        @pl.when(jnp.logical_not(is_owner))
        def _():
            step(OWNERS - 1, 0)

    def to_lines(send, recv, k):
        def step(i, _):
            other = ids[i]
            remote(
                send.at[other], recv.at[my_p], send_sems.at[k], recv_sems.at[k], other
            ).start()
            return 0

        lax.fori_loop(0, DEVS - 2, step, 0, unroll=6)
        step(DEVS - 2, 0)
        pltpu.make_async_copy(send.at[me], recv.at[my_p], recv_sems.at[k]).start()

    def tables_at(k):
        return tab[2 * k][...], tab[2 * k + 1][...]

    pairs_ref, x_twist_ref, y_twist_ref = tab[16:19]

    def forward_x(phys, send):
        re, im = x_forward(phys, tables_at(0), tables_at(1), (x_twist_ref[0], x_twist_ref[1]))
        put(send, 0, re)
        put(send, 1, im)

    def inverse_x(recv, j):
        re, im = get(recv, 2 * j, OWN_PAD), get(recv, 2 * j + 1, OWN_PAD)
        return x_inverse(re, im, tables_at(2), tables_at(3), (x_twist_ref[0], x_twist_ref[1]))

    def forward_y(recv):
        re, im = get(recv, 0, DEVS), get(recv, 1, DEVS)
        return y_forward(re, im, tables_at(4), tables_at(5), (y_twist_ref[0], y_twist_ref[1]))

    def inverse_y(re, im, send, j):
        re, im = y_inverse(re, im, tables_at(6), tables_at(7), (y_twist_ref[0], y_twist_ref[1]))
        put(send, 2 * j, re)
        put(send, 2 * j + 1, im)

    for load in loads:
        load.wait()

    wait_bytes(lines.at[0], recv_sems.at[0])
    forward_x(jnp.transpose(lines[0].reshape(LANES, 256)), send1)
    to_owners(send1, recv1, 2)
    wait_bytes(lines.at[1], recv_sems.at[1])
    fields[1] = jnp.transpose(lines[1].reshape(LANES, 256))
    forward_x(fields[1], send1b)
    to_owners(send1b, recv1b, 3)

    vel_copy.wait()
    lane = lax.broadcasted_iota(jnp.int32, (64, LANES), 1)
    line = lax.broadcasted_iota(jnp.int32, (64, LANES), 0)
    pack_y[0] = vel[:, 63, :]
    pack_y[1] = vel[:, 0, :]

    def pack(b, carry):
        last, first = carry
        value = vel[b]
        last = jnp.where(lane == b, pltpu.roll(value, b + 1, axis=1), last)
        first = jnp.where(lane == b, pltpu.roll(value, b, axis=1), first)
        return last, first

    zero = jnp.zeros((64, LANES), F32)
    last, first = lax.fori_loop(0, 3 * LZ, pack, (zero, zero))
    pack_x[0] = last
    pack_x[1] = first
    up_r, down_r = (row + 1) % ROWS, (row + ROWS - 1) % ROWS
    up_c, down_c = (col + 1) % COLS, (col + COLS - 1) % COLS
    halos = [
        remote(pack_y.at[0], low_y, halo_sems.at[0], halo_sems.at[4], up_r * COLS + col),
        remote(pack_y.at[1], high_y, halo_sems.at[1], halo_sems.at[5], down_r * COLS + col),
        remote(pack_x.at[0], low_x, halo_sems.at[2], halo_sems.at[6], row * COLS + up_c),
        remote(pack_x.at[1], high_x, halo_sems.at[3], halo_sems.at[7], row * COLS + down_c),
    ]
    for h in halos:
        h.start()

    @pl.when(is_owner)
    def _():
        kx, ky, mag, weight = wave_grids(my_p)
        wait_bytes(recv1, recv_sems.at[2])
        re, im = forward_y(recv1)
        spec[0] = re * weight
        spec[1] = im * weight
        inverse_y(spec[0] * mag, spec[1] * mag, send2, 0)
        to_lines(send2, recv2, 4)
        square = mag * mag
        inverse_y(spec[0] * square, spec[1] * square, send2b, 0)
        inverse_y(-kx * spec[1], kx * spec[0], send2b, 1)
        inverse_y(-ky * spec[1], ky * spec[0], send2b, 2)
        to_lines(send2b, recv2b, 5)
        wait_bytes(recv1b, recv_sems.at[3])
        re, im = forward_y(recv1b)
        spec[2] = re * weight
        spec[3] = im * weight
        cube = square * mag
        inverse_y(spec[0] * cube, spec[1] * cube, send2c, 0)
        inverse_y(-kx * spec[3], kx * spec[2], send2c, 1)
        inverse_y(-ky * spec[3], ky * spec[2], send2c, 2)
        to_lines(send2c, recv2c, 6)

    wait_bytes(recv2.at[:OWNERS], recv_sems.at[4])
    vert = inverse_x(recv2, 0)
    fields[2] = vert
    forward_x(-fields[1] * vert, send3)
    to_owners(send3, recv3, 7)

    def coarsen(j):
        hi, lo = split(out_t[j])
        spec[4] = dot(hi, pairs_ref[...]) + dot(lo, pairs_ref[...])
        return spec[4, pl.ds(0, 64, stride=2), :] + spec[4, pl.ds(1, 64, stride=2), :]

    wait_bytes(recv2b.at[:OWNERS], recv_sems.at[5])
    fields[3] = inverse_x(recv2b, 0)
    for j in range(2):
        slope = inverse_x(recv2b, 1 + j)
        fields[5 + j] = slope
        out_t[j] = jnp.transpose(slope)
        coarse_t[j] = coarsen(j)

    def spread(k, src, dst):
        for i in (4, 5, 3, 6, 2, 7, 1):
            to = (col + i) % COLS
            remote(src(to), dst, out_sems.at[k], out_sems.at[6 + k], row * COLS + to).start()
        pltpu.make_async_copy(src(col), dst, out_sems.at[6 + k]).start()

    few = lambda k: lambda to: coarse_t.at[k, pl.ds(to * 8, 8), :]
    fine = lambda k: lambda to: out_t.at[k, pl.ds(to * LINES, LINES), :]
    my_few, my_fine = pl.ds(col * 8, 8), pl.ds(col * LINES, LINES)
    spread(2, few(0), su_tile.at[my_few, :])
    spread(3, few(1), sv_tile.at[my_few, :])

    @pl.when(is_owner)
    def _():
        kx, ky, mag, weight = wave_grids(my_p)
        wait_bytes(recv3, recv_sems.at[7])
        re, im = forward_y(recv3)
        factor = weight * mag
        spec[0] = re * factor
        spec[1] = im * factor
        inverse_y(spec[0], spec[1], send4, 0)
        to_lines(send4, recv4, 8)
        inverse_y(spec[0] * mag, spec[1] * mag, send4b, 0)
        to_lines(send4b, recv4b, 9)

    wait_bytes(recv2c.at[:OWNERS], recv_sems.at[6])
    fields[4] = inverse_x(recv2c, 0)
    fields[7] = inverse_x(recv2c, 1)
    fields[8] = inverse_x(recv2c, 2)

    wait_bytes(recv4.at[:OWNERS], recv_sems.at[8])
    vert_two = inverse_x(recv4, 0)
    eta = fields[1]
    fields[2] = fields[2] + vert_two
    forward_x(-eta * vert_two - 0.5 * eta * eta * fields[3], send5)
    to_owners(send5, recv5, 10)

    for h in halos:
        h.wait()
    wait_bytes(su_tile, out_sems.at[8])
    wait_bytes(sv_tile, out_sems.at[9])

    def derivs(q, l, top):
        b = q * LZ + l
        mid = vel[b]
        above = jnp.where(l == 0, top, vel[q * LZ + jnp.maximum(l - 1, 0)])
        below = vel[q * LZ + jnp.minimum(l + 1, LZ - 1)]
        east = jnp.where(
            lane == LANES - 1,
            pltpu.roll(high_x[...], LANES - 1 - b, axis=1),
            pltpu.roll(mid, LANES - 1, axis=1),
        )
        west = jnp.where(
            lane == 0,
            pltpu.roll(low_x[...], (LANES - b) % LANES, axis=1),
            pltpu.roll(mid, 1, axis=1),
        )
        north = jnp.where(line == 63, high_y[pl.ds(b, 1), :], pltpu.roll(mid, 63, axis=0))
        south = jnp.where(line == 0, low_y[pl.ds(b, 1), :], pltpu.roll(mid, 1, axis=0))
        lap = east + west + north + south + above + below - 6.0 * mid
        return mid, 0.5 * (east - west), 0.5 * (north - south), 0.5 * (above - below), lap

    def level(l, _):
        depth = jnp.full((64, LANES), l, jnp.int32).astype(F32) + 0.5
        drift_decay = jnp.exp(-2.0 * DECAY_RATE * depth)
        u, u_dx, u_dy, u_dz, u_lap = derivs(0, l, su_tile[...])
        v, v_dx, v_dy, v_dz, v_lap = derivs(1, l, sv_tile[...])
        w, w_dx, w_dy, w_dz, w_lap = derivs(2, l, jnp.zeros((64, LANES), F32))
        vort_x = w_dy - v_dz
        vort_y = u_dz - w_dx
        vort_z = v_dx - u_dy
        drift_u = su_tile[...] * drift_decay
        drift_v = sv_tile[...] * drift_decay

        def advance(mid, dx, dy, dz, lap, force):
            carried = u * dx + v * dy + w * dz
            return mid + FLOW_STEP * (-carried + VISCOSITY * lap + force)

        base[l] = advance(u, u_dx, u_dy, u_dz, u_lap, drift_v * vort_z)
        base[LZ + l] = advance(v, v_dx, v_dy, v_dz, v_lap, -drift_u * vort_z)
        base[2 * LZ + l] = advance(w, w_dx, w_dy, w_dz, w_lap, drift_u * vort_y - drift_v * vort_x)
        return 0

    lax.fori_loop(0, EARLY_LEVELS, level, 0)

    @pl.when(is_owner)
    def _():
        kx, ky, mag, weight = wave_grids(my_p)
        wait_bytes(recv5, recv_sems.at[10])
        re, im = forward_y(recv5)
        factor = weight * mag
        inverse_y(re * factor, im * factor, send6, 0)
        to_lines(send6, recv6, 11)

    lax.fori_loop(EARLY_LEVELS, LZ, level, 0)
    base_copy = pltpu.make_async_copy(base, base_out, load_sems.at[n_tab + 1])
    base_copy.start()
    wait_bytes(recv4b.at[:OWNERS], recv_sems.at[9])
    curve_two = inverse_x(recv4b, 0)
    eta = fields[1]
    fields[2] = fields[2] + eta * (fields[3] + curve_two) + 0.5 * eta * eta * fields[4]
    pot_dx, pot_dy, height_dx, height_dy = (fields[5 + j] for j in range(4))
    fields[7] = 1.0 + (height_dx * height_dx + height_dy * height_dy)
    fields[3] = -(height_dx * pot_dx + height_dy * pot_dy)
    fields[4] = -GRAVITY * eta - 0.5 * (pot_dx * pot_dx + pot_dy * pot_dy)

    wait_bytes(recv6.at[:OWNERS], recv_sems.at[11])
    vertical = fields[2] + inverse_x(recv6, 0)
    scaled = fields[7] * vertical
    height_rate = fields[3] + scaled
    out_t[2] = jnp.transpose(height_rate)
    spread(0, fine(2), height_out.at[my_fine, :])
    out_t[3] = jnp.transpose(fields[4] + 0.5 * scaled * vertical)
    spread(1, fine(3), pot_out.at[my_fine, :])
    out_t[4] = jnp.transpose(GRAVITY * (fields[1] + SURFACE_STEP * height_rate))
    pressure = coarsen(4)
    coarse_t[2] = pressure
    spread(5, few(2), press_out.at[pl.ds(col * 8 + 8, 8), :])

    @pl.when(col == COLS - 1)
    def _():
        for to in range(COLS):
            remote(
                coarse_t.at[2, pl.ds(to * 8, 8), :],
                press_out.at[pl.ds(0, 8), :],
                out_sems.at[12],
                out_sems.at[11],
                up_r * COLS + to,
            ).start()

    @pl.when(col == 0)
    def _():
        for to in range(COLS):
            remote(
                coarse_t.at[2, pl.ds(to * 8, 8), :],
                press_out.at[pl.ds(72, 8), :],
                out_sems.at[12],
                out_sems.at[11],
                down_r * COLS + to,
            ).start()

    east = pltpu.roll(pressure, LANES - 1, axis=1)
    east = jnp.where(lane == LANES - 1, pltpu.roll(east, 56, axis=0), east)
    west = pltpu.roll(pressure, 1, axis=1)
    west = jnp.where(lane == 0, pltpu.roll(west, 8, axis=0), west)
    coarse_t[3] = 0.5 * (east - west)
    spread(4, few(3), lx_out.at[my_few, :])

    for f in range(2):
        wait_bytes(lines.at[f, :7], send_sems.at[f])
    for k in range(2):
        wait_bytes(out_t.at[k, :112, :], out_sems.at[k])
    for k in range(4):
        wait_bytes(coarse_t.at[k, :56, :], out_sems.at[2 + k])

    @pl.when((col == 0) | (col == COLS - 1))
    def _():
        wait_bytes(coarse_t.at[2], out_sems.at[12])

    owned = ((send1, 2), (send1b, 3), (send3, 7), (send5, 10))

    @pl.when(is_owner)
    def _():
        for buf, k in owned:
            wait_bytes(buf.at[: OWNERS - 1], send_sems.at[k])
        for buf, k in (
            (send2, 4),
            (send2b, 5),
            (send2c, 6),
            (send4, 8),
            (send4b, 9),
            (send6, 11),
        ):
            wait_bytes(buf.at[: DEVS - 1], send_sems.at[k])

    @pl.when(jnp.logical_not(is_owner))
    def _():
        for buf, k in owned:
            wait_bytes(buf.at[:OWNERS], send_sems.at[k])

    base_copy.wait()
    for k, ref in ((0, height_out), (1, pot_out), (4, lx_out), (5, press_out)):
        wait_bytes(ref, out_sems.at[6 + k])


CHUNK = 8


def load_kernel(base_in, lx_in, press_in, height_in, pot_in, out, height_out, pot_out, *scratch):
    base, load_x_buf, press, height, pot, in_sems, done_sems = scratch
    small = [
        pltpu.make_async_copy(src, dst, in_sems.at[k])
        for k, (src, dst) in enumerate(
            ((lx_in, load_x_buf), (press_in, press), (height_in, height), (pot_in, pot))
        )
    ]
    for copy in small[:2]:
        copy.start()
    chunks = 3 * LZ // CHUNK
    parts = [pl.ds(CHUNK * k, CHUNK) for k in range(chunks)]
    ins = [pltpu.make_async_copy(base_in.at[p], base.at[p], in_sems.at[4 + k]) for k, p in enumerate(parts)]
    outs = [pltpu.make_async_copy(base.at[p], out.at[p], done_sems.at[2 + k]) for k, p in enumerate(parts)]
    for copy in ins:
        copy.start()
    for copy in small[2:]:
        copy.start()
    small[0].wait()
    small[1].wait()
    loads = (load_x_buf[...], 0.5 * (press[9:73, :] - press[7:71, :]))
    for k in range(chunks):
        ins[k].wait()
        for b in range(CHUNK * k, CHUNK * k + CHUNK):
            q, l = divmod(b, LZ)
            if q < 2:
                decay = float(np.exp(-DECAY_RATE * (l + 0.5)))
                base[b] = base[b] - (FLOW_STEP * decay) * loads[q]
        outs[k].start()
    small[2].wait()
    last = [
        pltpu.make_async_copy(height, height_out, done_sems.at[0]),
        pltpu.make_async_copy(pot, pot_out, done_sems.at[1]),
    ]
    last[0].start()
    small[3].wait()
    last[1].start()
    for copy in outs + last:
        copy.wait()


def local(surface_height, surface_potential, velocity):
    flow = velocity.reshape(3 * LZ, 64, LANES)
    tabs = [jnp.asarray(t) for t in tables()]
    anywhere = pl.BlockSpec(memory_space=pl.ANY)

    def shape(*dims):
        return jax.ShapeDtypeStruct(dims, F32)

    def buf(*dims):
        return VMEM(dims, F32)

    messages = []
    for kind, count in zip("oolllollol", (2, 2, 2, 6, 6, 2, 2, 2, 2, 2)):
        if kind == "o":
            messages += [buf(OWN_PAD, count, LANES), buf(DEVS, count, LANES)]
        else:
            messages += [buf(DEVS, count, LANES), buf(OWN_PAD, count, LANES)]
    outs = pl.pallas_call(
        surface_kernel,
        name="surface",
        out_shape=[
            shape(128, 256),
            shape(128, 256),
            shape(64, LANES),
            shape(80, LANES),
            shape(3 * LZ, 64, LANES),
        ],
        in_specs=[anywhere] * (3 + len(tabs)),
        out_specs=[anywhere] * 5,
        scratch_shapes=[VMEM(t.shape, t.dtype) for t in tabs]
        + [buf(2, COLS, LINES, 256), buf(9, 256, LANES)]
        + messages
        + [
            buf(5, LANES, LANES),
            buf(5, LANES, 256),
            buf(4, 64, LANES),
            buf(3 * LZ, 64, LANES),
            buf(3 * LZ, 64, LANES),
            buf(2, 48, LANES),
            buf(2, 64, LANES),
            buf(48, LANES),
            buf(48, LANES),
            buf(64, LANES),
            buf(64, LANES),
            buf(64, LANES),
            buf(64, LANES),
            pltpu.SMEM((DEVS,), jnp.int32),
            pltpu.SMEM((DEVS,), jnp.int32),
            pltpu.SMEM((DEVS,), jnp.int32),
            pltpu.SemaphoreType.DMA((len(tabs) + 2,)),
            pltpu.SemaphoreType.DMA((12,)),
            pltpu.SemaphoreType.DMA((12,)),
            pltpu.SemaphoreType.DMA((13,)),
            pltpu.SemaphoreType.DMA((8,)),
        ],
        compiler_params=pltpu.CompilerParams(
            collective_id=0, has_side_effects=True, vmem_limit_bytes=56 * 1024 * 1024
        ),
    )(surface_potential, surface_height, flow, *tabs)
    height_rate, potential_rate, lx, press, base = outs
    nxt, height_rate, potential_rate = pl.pallas_call(
        load_kernel,
        name="load",
        out_shape=[shape(3 * LZ, 64, LANES), shape(128, 256), shape(128, 256)],
        in_specs=[anywhere] * 5,
        out_specs=[anywhere] * 3,
        scratch_shapes=[
            buf(3 * LZ, 64, LANES),
            buf(64, LANES),
            buf(80, LANES),
            buf(128, 256),
            buf(128, 256),
            pltpu.SemaphoreType.DMA((4 + 3 * LZ // CHUNK,)),
            pltpu.SemaphoreType.DMA((2 + 3 * LZ // CHUNK,)),
        ],
    )(base, lx, press, height_rate, potential_rate)
    return height_rate, potential_rate, nxt.reshape(velocity.shape)


def solution(mesh):
    specs = (P("row", "col"), P("row", "col"), P(None, None, "row", "col"))
    return jax.shard_map(local, mesh=mesh, in_specs=specs, out_specs=specs, check_vma=False)
```

time: 101 us -> 71.9 us (0.71)
  Pallas kernels: 92.1 us -> 71 us
  local copies, waits for them, and re-layouts: 7.35 us -> 0 us
    pallas_call x1, Pallas kernels: 87.7 us -> 68.6 us  [local(): pl.pallas_call(surface_kernel, name='surface', out_shape=[shape(128, 256)...]
    unnamed x24 -> x0, local copies, waits for them, and re-layouts: 7.35 us -> none
    pallas_call x1, Pallas kernels: 4.42 us -> 2.39 us  [local(): pl.pallas_call(load_kernel, name='load', out_shape=[shape(3 * LZ, 64, LAN...]
where the time goes in v2:
time: 71.9 us; the launch traced here: 71.8 us
  Pallas kernels  71 us (99%)
  between operations  0.8 us (1%)
    pallas_call x1, Pallas kernels, local(): pl.pallas_call(surface_kernel, name='surface', out_shape=[shape(128, 256)...  68.6 us
    pallas_call x1, Pallas kernels, local(): pl.pallas_call(load_kernel, name='load', out_shape=[shape(3 * LZ, 64, LAN...  2.39 us

profile of v2, /device:TPU:1, one launch (start us, length us, event | category | flops | bytes accessed | tf_op | source)
XLA Modules:
  0.0 71.8 jit_solution(18008375801383259046)
XLA Ops:
  0.6 68.6 %surface.1 = (f32[128,256]{1,0:T(8,128)}, f32[128,256]{1,0:T(8,128)}, f32[64,128]{1,0:T(8,128)}, f32[80,128]{1,0:T(8,128)}, f32[48,64,128]{2,1,0:T(8,128)}) custom-call(f32[128,256]{1,0:T(8,128)} %refs_0_.1, f32[128,256]{1,0:T(8,128)} %refs_1_.1, f32[48,64,128]{2,1,0:T(8,128)} %bitcast.2, bf16[128,256]{1,0:T(8,128)(2,1)} %constant.38.clone.refs_3_, ...), custom_call_target="tpu_custom_call" | custom-call | tf_op jit(solution)/shard_map/surface/pallas_call | solution.py:671
  69.2 2.4 %load.1 = (f32[48,64,128]{2,1,0:T(8,128)}, f32[128,256]{1,0:T(8,128)}, f32[128,256]{1,0:T(8,128)}) custom-call(f32[48,64,128]{2,1,0:T(8,128)} %get-tuple-element.11.base_in, f32[64,128]{1,0:T(8,128)} %get-tuple-element.12.lx_in, f32[80,128]{1,0:T(8,128)} %get-tuple-element.13.press_in, f32[128,256]{1,0:T(8,128)} %get-tuple-element.14.height_in, ...), custom_call_target="tpu_custom_call" | custom-call | tf_op jit(solution)/shard_map/load/pallas_call | solution.py:714

commit v3 on v2

--- a/solution.py
+++ b/solution.py
@@ -24,7 +24,9 @@
 VISCOSITY = 0.2
 DECAY_RATE = 0.05
 LOGICAL = pl.DeviceIdType.LOGICAL
-EARLY_LEVELS = 8
+EARLY_LEVELS = 12
+SURFACE_VMEM = 20 * 1024 * 1024
+LOAD_VMEM = 8 * 1024 * 1024
 F32 = jnp.float32
 BF16 = jnp.bfloat16
 VMEM = pltpu.VMEM
@@ -58,15 +60,13 @@
     x_third = block_complex(cp.T, sp.T)
     c1, s1 = wave(r128, r128, 128)
     y_first = block_complex(c1, -s1)
-    y_last = block_complex(c1, s1)
     y_second = block_complex(np.kron(eye8, c16), np.kron(eye8, s16))
-    y_third = block_complex(np.kron(eye8, c16), np.kron(eye8, -s16))
     ct, st = wave(r256, r8, N)
     x_twist = np.stack([np.repeat(ct, 16, axis=1), np.repeat(st, 16, axis=1)])
     ct, st = wave(r128, r16, N)
     y_twist = np.stack([np.tile(ct, (1, 8)), np.tile(st, (1, 8))])
     pairs = np.kron(np.eye(128), np.ones((2, 1))) * 0.25
-    mats = [x_first, x_second, x_third, x_last, y_first, y_second, y_third, y_last]
+    mats = [x_first, x_second, x_third, x_last, y_first, y_second]
     out = []
     for m in mats:
         out.extend(split_table(m))
@@ -88,7 +88,9 @@
 def left_table(table, data):
     th, tl = table
     dh, dl = split(data)
-    return dot(th, dh) + dot(th, dl) + dot(tl, dh)
+    both = dot(th, jnp.concatenate([dh, dl], axis=1))
+    width = data.shape[1]
+    return both[:, :width] + both[:, width:] + dot(tl, dh)
 
 
 def right_table(data, table):
@@ -122,12 +124,12 @@
     return z[:, :LANES], z[:, LANES:]
 
 
-def y_inverse(re, im, third, last, twist):
-    u = right_table(jnp.concatenate([re, im], axis=1), third)
+def y_inverse(re, im, first, second, twist):
+    u = right_table(jnp.concatenate([re, -im], axis=1), second)
     ur, ui = u[:, :LANES], u[:, LANES:]
     c, s = twist
-    out = left_table(last, jnp.concatenate([ur * c - ui * s, ur * s + ui * c], axis=0))
-    return out[:LANES], out[LANES:]
+    out = left_table(first, jnp.concatenate([ur * c + ui * s, ui * c - ur * s], axis=0))
+    return out[:LANES], -out[LANES:]
 
 
 def wave_grids(p):
@@ -161,11 +163,19 @@
 
 def surface_kernel(*refs):
     phi_ref, eta_ref, vel_ref = refs[:3]
-    n_tab = 19
+    n_tab = 15
     tab_in = refs[3 : 3 + n_tab]
     at = 3 + n_tab
-    height_out, pot_out, lx_out, press_out, base_out = refs[at : at + 5]
-    at += 5
+    (
+        height_out,
+        lx_out,
+        press_out,
+        base_out,
+        stretch_out,
+        advected_out,
+        still_out,
+    ) = refs[at : at + 7]
+    at += 7
     tab = refs[at : at + n_tab]
     at += n_tab
     (
@@ -181,6 +191,8 @@
         recv2b,
         send2c,
         recv2c,
+        send2d,
+        recv2d,
         send3,
         recv3,
         send4,
@@ -211,6 +223,7 @@
         send_sems,
         recv_sems,
         out_sems,
+        early_sems,
         halo_sems,
     ) = refs[at:]
     row, col = lax.axis_index("row"), lax.axis_index("col")
@@ -248,6 +261,22 @@
     ]
     for load in loads:
         load.start()
+
+    pl.semaphore_wait(barrier, COLS + ROWS - 2)
+
+    for f, ref in enumerate((phi_ref, eta_ref)):
+        for i in (5, 3, 7, 1, 4, 6, 2):
+            to = (col + i) % COLS
+            remote(
+                ref.at[pl.ds(to * LINES, LINES), :],
+                lines.at[f, col],
+                send_sems.at[f],
+                recv_sems.at[f],
+                row * COLS + to,
+            ).start()
+        pltpu.make_async_copy(
+            ref.at[pl.ds(col * LINES, LINES), :], lines.at[f, col], recv_sems.at[f]
+        ).start()
 
     x_at = (col % 2) * 2 + row // 8
     y_at = (row // 2) % 4
@@ -270,24 +299,8 @@
             slot = slot + (place - 3 * third < 2).astype(jnp.int32)
             entry += 1
 
-    for buf in (recv2, recv2b, recv2c, recv4, recv4b, recv6):
+    for buf in (recv2, recv2b, recv2c, recv2d, recv4, recv4b, recv6):
         buf[OWNERS:OWN_PAD] = jnp.zeros((OWN_PAD - OWNERS,) + buf.shape[1:], F32)
-    pl.semaphore_wait(barrier, COLS + ROWS - 2)
-
-    for f, ref in enumerate((phi_ref, eta_ref)):
-        for i in (4, 5, 3, 6, 2, 7, 1):
-            to = (col + i) % COLS
-            remote(
-                ref.at[pl.ds(to * LINES, LINES), :],
-                lines.at[f, col],
-                send_sems.at[f],
-                recv_sems.at[f],
-                row * COLS + to,
-            ).start()
-        pltpu.make_async_copy(
-            ref.at[pl.ds(col * LINES, LINES), :], lines.at[f, col], recv_sems.at[f]
-        ).start()
-
     def to_owners(send, recv, k):
         def step(i, _):
             remote(
@@ -320,7 +333,7 @@
     def tables_at(k):
         return tab[2 * k][...], tab[2 * k + 1][...]
 
-    pairs_ref, x_twist_ref, y_twist_ref = tab[16:19]
+    pairs_ref, x_twist_ref, y_twist_ref = tab[12:15]
 
     def forward_x(phys, send):
         re, im = x_forward(phys, tables_at(0), tables_at(1), (x_twist_ref[0], x_twist_ref[1]))
@@ -336,7 +349,7 @@
         return y_forward(re, im, tables_at(4), tables_at(5), (y_twist_ref[0], y_twist_ref[1]))
 
     def inverse_y(re, im, send, j):
-        re, im = y_inverse(re, im, tables_at(6), tables_at(7), (y_twist_ref[0], y_twist_ref[1]))
+        re, im = y_inverse(re, im, tables_at(4), tables_at(5), (y_twist_ref[0], y_twist_ref[1]))
         put(send, 2 * j, re)
         put(send, 2 * j + 1, im)
 
@@ -365,7 +378,7 @@
         return last, first
 
     zero = jnp.zeros((64, LANES), F32)
-    last, first = lax.fori_loop(0, 3 * LZ, pack, (zero, zero))
+    last, first = lax.fori_loop(0, 3 * LZ, pack, (zero, zero), unroll=8)
     pack_x[0] = last
     pack_x[1] = first
     up_r, down_r = (row + 1) % ROWS, (row + ROWS - 1) % ROWS
@@ -390,18 +403,17 @@
         to_lines(send2, recv2, 4)
         square = mag * mag
         inverse_y(spec[0] * square, spec[1] * square, send2b, 0)
-        inverse_y(-kx * spec[1], kx * spec[0], send2b, 1)
-        inverse_y(-ky * spec[1], ky * spec[0], send2b, 2)
         to_lines(send2b, recv2b, 5)
+        inverse_y(-kx * spec[1], kx * spec[0], send2c, 0)
+        inverse_y(-ky * spec[1], ky * spec[0], send2c, 1)
         wait_bytes(recv1b, recv_sems.at[3])
         re, im = forward_y(recv1b)
         spec[2] = re * weight
         spec[3] = im * weight
+        inverse_y(-kx * spec[3], kx * spec[2], send2c, 2)
+        inverse_y(-ky * spec[3], ky * spec[2], send2c, 3)
         cube = square * mag
-        inverse_y(spec[0] * cube, spec[1] * cube, send2c, 0)
-        inverse_y(-kx * spec[3], kx * spec[2], send2c, 1)
-        inverse_y(-ky * spec[3], ky * spec[2], send2c, 2)
-        to_lines(send2c, recv2c, 6)
+        inverse_y(spec[0] * cube, spec[1] * cube, send2d, 0)
 
     wait_bytes(recv2.at[:OWNERS], recv_sems.at[4])
     vert = inverse_x(recv2, 0)
@@ -409,30 +421,12 @@
     forward_x(-fields[1] * vert, send3)
     to_owners(send3, recv3, 7)
 
-    def coarsen(j):
-        hi, lo = split(out_t[j])
-        spec[4] = dot(hi, pairs_ref[...]) + dot(lo, pairs_ref[...])
-        return spec[4, pl.ds(0, 64, stride=2), :] + spec[4, pl.ds(1, 64, stride=2), :]
+    @pl.when(is_owner)
+    def _():
+        to_lines(send2c, recv2c, 6)
 
     wait_bytes(recv2b.at[:OWNERS], recv_sems.at[5])
     fields[3] = inverse_x(recv2b, 0)
-    for j in range(2):
-        slope = inverse_x(recv2b, 1 + j)
-        fields[5 + j] = slope
-        out_t[j] = jnp.transpose(slope)
-        coarse_t[j] = coarsen(j)
-
-    def spread(k, src, dst):
-        for i in (4, 5, 3, 6, 2, 7, 1):
-            to = (col + i) % COLS
-            remote(src(to), dst, out_sems.at[k], out_sems.at[6 + k], row * COLS + to).start()
-        pltpu.make_async_copy(src(col), dst, out_sems.at[6 + k]).start()
-
-    few = lambda k: lambda to: coarse_t.at[k, pl.ds(to * 8, 8), :]
-    fine = lambda k: lambda to: out_t.at[k, pl.ds(to * LINES, LINES), :]
-    my_few, my_fine = pl.ds(col * 8, 8), pl.ds(col * LINES, LINES)
-    spread(2, few(0), su_tile.at[my_few, :])
-    spread(3, few(1), sv_tile.at[my_few, :])
 
     @pl.when(is_owner)
     def _():
@@ -447,10 +441,37 @@
         inverse_y(spec[0] * mag, spec[1] * mag, send4b, 0)
         to_lines(send4b, recv4b, 9)
 
+    def coarsen(j):
+        hi, lo = split(out_t[j])
+        spec[4] = dot(hi, pairs_ref[...]) + dot(lo, pairs_ref[...])
+        return spec[4, pl.ds(0, 64, stride=2), :] + spec[4, pl.ds(1, 64, stride=2), :]
+
     wait_bytes(recv2c.at[:OWNERS], recv_sems.at[6])
-    fields[4] = inverse_x(recv2c, 0)
-    fields[7] = inverse_x(recv2c, 1)
-    fields[8] = inverse_x(recv2c, 2)
+    for j in range(2):
+        slope = inverse_x(recv2c, j)
+        fields[5 + j] = slope
+        out_t[j] = jnp.transpose(slope)
+        coarse_t[j] = coarsen(j)
+
+    def spread_with(send_sem, recv_sem, src, dst):
+        for i in (5, 3, 7, 1, 4, 6, 2):
+            to = (col + i) % COLS
+            remote(src(to), dst, send_sem, recv_sem, row * COLS + to).start()
+        pltpu.make_async_copy(src(col), dst, recv_sem).start()
+
+    def spread(k, src, dst):
+        spread_with(out_sems.at[k], out_sems.at[6 + k], src, dst)
+
+    def spread_early(k, src, dst):
+        spread_with(early_sems.at[k], early_sems.at[3 + k], src, dst)
+
+    few = lambda k: lambda to: coarse_t.at[k, pl.ds(to * 8, 8), :]
+    fine = lambda k: lambda to: out_t.at[k, pl.ds(to * LINES, LINES), :]
+    my_few, my_fine = pl.ds(col * 8, 8), pl.ds(col * LINES, LINES)
+    spread(2, few(0), su_tile.at[my_few, :])
+    spread(3, few(1), sv_tile.at[my_few, :])
+    fields[7] = inverse_x(recv2c, 2)
+    fields[8] = inverse_x(recv2c, 3)
 
     wait_bytes(recv4.at[:OWNERS], recv_sems.at[8])
     vert_two = inverse_x(recv4, 0)
@@ -458,6 +479,20 @@
     fields[2] = fields[2] + vert_two
     forward_x(-eta * vert_two - 0.5 * eta * eta * fields[3], send5)
     to_owners(send5, recv5, 10)
+
+    @pl.when(is_owner)
+    def _():
+        to_lines(send2d, recv2d, 12)
+
+    pot_dx, pot_dy, height_dx, height_dy = (fields[5 + j] for j in range(4))
+    stretch = 1.0 + (height_dx * height_dx + height_dy * height_dy)
+    advected = -(height_dx * pot_dx + height_dy * pot_dy)
+    fields[7] = stretch
+    fields[8] = advected
+    out_t[0] = jnp.transpose(stretch)
+    spread_early(0, fine(0), stretch_out.at[my_fine, :])
+    out_t[1] = jnp.transpose(advected)
+    spread_early(1, fine(1), advected_out.at[my_fine, :])
 
     for h in halos:
         h.wait()
@@ -516,26 +551,24 @@
         inverse_y(re * factor, im * factor, send6, 0)
         to_lines(send6, recv6, 11)
 
+    eta = fields[1]
+    pot_dx, pot_dy = fields[5], fields[6]
+    out_t[2] = jnp.transpose(-GRAVITY * eta - 0.5 * (pot_dx * pot_dx + pot_dy * pot_dy))
+    spread_early(2, fine(2), still_out.at[my_fine, :])
     lax.fori_loop(EARLY_LEVELS, LZ, level, 0)
     base_copy = pltpu.make_async_copy(base, base_out, load_sems.at[n_tab + 1])
     base_copy.start()
+    wait_bytes(recv2d.at[:OWNERS], recv_sems.at[12])
+    cube_one = inverse_x(recv2d, 0)
     wait_bytes(recv4b.at[:OWNERS], recv_sems.at[9])
     curve_two = inverse_x(recv4b, 0)
     eta = fields[1]
-    fields[2] = fields[2] + eta * (fields[3] + curve_two) + 0.5 * eta * eta * fields[4]
-    pot_dx, pot_dy, height_dx, height_dy = (fields[5 + j] for j in range(4))
-    fields[7] = 1.0 + (height_dx * height_dx + height_dy * height_dy)
-    fields[3] = -(height_dx * pot_dx + height_dy * pot_dy)
-    fields[4] = -GRAVITY * eta - 0.5 * (pot_dx * pot_dx + pot_dy * pot_dy)
+    fields[2] = fields[2] + eta * (fields[3] + curve_two) + 0.5 * eta * eta * cube_one
 
     wait_bytes(recv6.at[:OWNERS], recv_sems.at[11])
-    vertical = fields[2] + inverse_x(recv6, 0)
-    scaled = fields[7] * vertical
-    height_rate = fields[3] + scaled
-    out_t[2] = jnp.transpose(height_rate)
-    spread(0, fine(2), height_out.at[my_fine, :])
-    out_t[3] = jnp.transpose(fields[4] + 0.5 * scaled * vertical)
-    spread(1, fine(3), pot_out.at[my_fine, :])
+    height_rate = fields[8] + fields[7] * (fields[2] + inverse_x(recv6, 0))
+    out_t[3] = jnp.transpose(height_rate)
+    spread(0, fine(3), height_out.at[my_fine, :])
     out_t[4] = jnp.transpose(GRAVITY * (fields[1] + SURFACE_STEP * height_rate))
     pressure = coarsen(4)
     coarse_t[2] = pressure
@@ -572,8 +605,9 @@
 
     for f in range(2):
         wait_bytes(lines.at[f, :7], send_sems.at[f])
-    for k in range(2):
-        wait_bytes(out_t.at[k, :112, :], out_sems.at[k])
+    wait_bytes(out_t.at[3, :112, :], out_sems.at[0])
+    for k in range(3):
+        wait_bytes(out_t.at[k, :112, :], early_sems.at[k])
     for k in range(4):
         wait_bytes(coarse_t.at[k, :56, :], out_sems.at[2 + k])
 
@@ -591,6 +625,7 @@
             (send2, 4),
             (send2b, 5),
             (send2c, 6),
+            (send2d, 12),
             (send4, 8),
             (send4b, 9),
             (send6, 11),
@@ -603,52 +638,45 @@
             wait_bytes(buf.at[:OWNERS], send_sems.at[k])
 
     base_copy.wait()
-    for k, ref in ((0, height_out), (1, pot_out), (4, lx_out), (5, press_out)):
+    for k, ref in enumerate((stretch_out, advected_out, still_out)):
+        wait_bytes(ref, early_sems.at[3 + k])
+    for k, ref in ((0, height_out), (4, lx_out), (5, press_out)):
         wait_bytes(ref, out_sems.at[6 + k])
 
 
 CHUNK = 8
 
 
-def load_kernel(base_in, lx_in, press_in, height_in, pot_in, out, height_out, pot_out, *scratch):
-    base, load_x_buf, press, height, pot, in_sems, done_sems = scratch
-    small = [
-        pltpu.make_async_copy(src, dst, in_sems.at[k])
-        for k, (src, dst) in enumerate(
-            ((lx_in, load_x_buf), (press_in, press), (height_in, height), (pot_in, pot))
-        )
+def load_kernel(*refs):
+    load_x, press, height, stretch, advected, still, base = refs[:7]
+    out, height_out, pot_out = refs[7:10]
+    stage, pot, sems = refs[10:]
+    straight = [
+        pltpu.make_async_copy(height, height_out, sems.at[0]),
+        pltpu.make_async_copy(base.at[pl.ds(2 * LZ, LZ)], out.at[pl.ds(2 * LZ, LZ)], sems.at[1]),
     ]
-    for copy in small[:2]:
+    for copy in straight:
         copy.start()
-    chunks = 3 * LZ // CHUNK
-    parts = [pl.ds(CHUNK * k, CHUNK) for k in range(chunks)]
-    ins = [pltpu.make_async_copy(base_in.at[p], base.at[p], in_sems.at[4 + k]) for k, p in enumerate(parts)]
-    outs = [pltpu.make_async_copy(base.at[p], out.at[p], done_sems.at[2 + k]) for k, p in enumerate(parts)]
-    for copy in ins:
-        copy.start()
-    for copy in small[2:]:
-        copy.start()
-    small[0].wait()
-    small[1].wait()
-    loads = (load_x_buf[...], 0.5 * (press[9:73, :] - press[7:71, :]))
-    for k in range(chunks):
-        ins[k].wait()
+    loads = (load_x[...], 0.5 * (press[9:73, :] - press[7:71, :]))
+    outs = []
+    for k in range(2 * LZ // CHUNK):
         for b in range(CHUNK * k, CHUNK * k + CHUNK):
             q, l = divmod(b, LZ)
-            if q < 2:
-                decay = float(np.exp(-DECAY_RATE * (l + 0.5)))
-                base[b] = base[b] - (FLOW_STEP * decay) * loads[q]
-        outs[k].start()
-    small[2].wait()
-    last = [
-        pltpu.make_async_copy(height, height_out, done_sems.at[0]),
-        pltpu.make_async_copy(pot, pot_out, done_sems.at[1]),
-    ]
-    last[0].start()
-    small[3].wait()
-    last[1].start()
-    for copy in outs + last:
+            decay = float(np.exp(-DECAY_RATE * (l + 0.5)))
+            stage[b] = base[b] - (FLOW_STEP * decay) * loads[q]
+        part = pl.ds(CHUNK * k, CHUNK)
+        outs.append(pltpu.make_async_copy(stage.at[part], out.at[part], sems.at[3 + k]))
+        outs[-1].start()
+    lifted = height[...] - advected[...]
+    pot[...] = still[...] + 0.5 * lifted * (lifted / stretch[...])
+    outs.append(pltpu.make_async_copy(pot, pot_out, sems.at[2]))
+    outs[-1].start()
+    for copy in straight + outs:
         copy.wait()
+
+
+def in_hbm(a):
+    return pltpu.with_memory_space_constraint(a, pltpu.HBM)
 
 
 def local(surface_height, surface_potential, velocity):
@@ -663,7 +691,7 @@
         return VMEM(dims, F32)
 
     messages = []
-    for kind, count in zip("oolllollol", (2, 2, 2, 6, 6, 2, 2, 2, 2, 2)):
+    for kind, count in zip("oollllollol", (2, 2, 2, 2, 8, 2, 2, 2, 2, 2, 2)):
         if kind == "o":
             messages += [buf(OWN_PAD, count, LANES), buf(DEVS, count, LANES)]
         else:
@@ -673,13 +701,15 @@
         name="surface",
         out_shape=[
             shape(128, 256),
-            shape(128, 256),
             shape(64, LANES),
             shape(80, LANES),
             shape(3 * LZ, 64, LANES),
+            shape(128, 256),
+            shape(128, 256),
+            shape(128, 256),
         ],
         in_specs=[anywhere] * (3 + len(tabs)),
-        out_specs=[anywhere] * 5,
+        out_specs=[anywhere] * 7,
         scratch_shapes=[VMEM(t.shape, t.dtype) for t in tabs]
         + [buf(2, COLS, LINES, 256), buf(9, 256, LANES)]
         + messages
@@ -701,32 +731,30 @@
             pltpu.SMEM((DEVS,), jnp.int32),
             pltpu.SMEM((DEVS,), jnp.int32),
             pltpu.SemaphoreType.DMA((len(tabs) + 2,)),
-            pltpu.SemaphoreType.DMA((12,)),
-            pltpu.SemaphoreType.DMA((12,)),
             pltpu.SemaphoreType.DMA((13,)),
+            pltpu.SemaphoreType.DMA((13,)),
+            pltpu.SemaphoreType.DMA((13,)),
+            pltpu.SemaphoreType.DMA((6,)),
             pltpu.SemaphoreType.DMA((8,)),
         ],
         compiler_params=pltpu.CompilerParams(
-            collective_id=0, has_side_effects=True, vmem_limit_bytes=56 * 1024 * 1024
+            collective_id=0, has_side_effects=True, vmem_limit_bytes=SURFACE_VMEM
         ),
-    )(surface_potential, surface_height, flow, *tabs)
-    height_rate, potential_rate, lx, press, base = outs
+    )(*(in_hbm(a) for a in (surface_potential, surface_height, flow, *tabs)))
+    height_rate, lx, press, base, stretch, advected, still = outs
     nxt, height_rate, potential_rate = pl.pallas_call(
         load_kernel,
         name="load",
         out_shape=[shape(3 * LZ, 64, LANES), shape(128, 256), shape(128, 256)],
-        in_specs=[anywhere] * 5,
+        in_specs=[pl.BlockSpec(memory_space=VMEM)] * 7,
         out_specs=[anywhere] * 3,
         scratch_shapes=[
-            buf(3 * LZ, 64, LANES),
-            buf(64, LANES),
-            buf(80, LANES),
+            buf(2 * LZ, 64, LANES),
             buf(128, 256),
-            buf(128, 256),
-            pltpu.SemaphoreType.DMA((4 + 3 * LZ // CHUNK,)),
-            pltpu.SemaphoreType.DMA((2 + 3 * LZ // CHUNK,)),
+            pltpu.SemaphoreType.DMA((3 + 2 * LZ // CHUNK,)),
         ],
-    )(base, lx, press, height_rate, potential_rate)
+        compiler_params=pltpu.CompilerParams(vmem_limit_bytes=LOAD_VMEM),
+    )(lx, press, height_rate, stretch, advected, still, base)
     return height_rate, potential_rate, nxt.reshape(velocity.shape)
 
 

time: 71.9 us -> 65 us (0.904)
  Pallas kernels: 71 us -> 64.3 us
    pallas_call x1, Pallas kernels: 68.6 us -> 63 us  [local(): pl.pallas_call(surface_kernel, name='surface', out_shape=[shape(128, 256)...]
    pallas_call x1, Pallas kernels: 2.39 us -> 1.28 us  [local(): pl.pallas_call(load_kernel, name='load', out_shape=[shape(3 * LZ, 64, LAN...]
where the time goes in v3:
time: 65 us; the launch traced here: 64.9 us
  Pallas kernels  64.3 us (99%)
    pallas_call x1, Pallas kernels, local(): pl.pallas_call(surface_kernel, name='surface', out_shape=[shape(128, 256)...  63 us

profile of v3, /device:TPU:1, one launch (start us, length us, event | category | flops | bytes accessed | tf_op | source)
XLA Modules:
  0.0 64.9 jit_solution(10734138783138826233)
XLA Ops:
  0.6 63.0 %surface.1 = (f32[128,256]{1,0:T(8,128)S(1)}, f32[64,128]{1,0:T(8,128)S(1)}, f32[80,128]{1,0:T(8,128)S(1)}, f32[48,64,128]{2,1,0:T(8,128)S(1)}, f32[128,256]{1,0...) custom-call(f32[128,256]{1,0:T(8,128)} %refs_0_.1, f32[128,256]{1,0:T(8,128)} %refs_1_.1, ...), custom_call_target="tpu_custom_call" | custom-call | tf_op jit(solution)/shard_map/surface/pallas_call | solution.py:699
  63.6 1.3 %load.1 = (f32[48,64,128]{2,1,0:T(8,128)}, f32[128,256]{1,0:T(8,128)}, f32[128,256]{1,0:T(8,128)}) custom-call(f32[64,128]{1,0:T(8,128)S(1)} %get-tuple-element.13.refs_0_, f32[80,128]{1,0:T(8,128)S(1)} %get-tuple-element.14.refs_1_, f32[128,256]{1,0:T(8,128)S(1)} %get-tuple-element.15.refs_2_, f32[128,256]{1,0:T(8,128)S(1)} %get-tuple-element.16.refs_3_, ...), custom_call_target="tpu_custom_call" | custom-call | tf_op jit(solution)/shard_map/load/pallas_call | solution.py:745

commit v4 on v3

--- a/solution.py
+++ b/solution.py
@@ -68,8 +68,14 @@
     pairs = np.kron(np.eye(128), np.ones((2, 1))) * 0.25
     mats = [x_first, x_second, x_third, x_last, y_first, y_second]
     out = []
-    for m in mats:
-        out.extend(split_table(m))
+    for k, m in enumerate(mats):
+        hi, lo = split_table(m)
+        if k == 0:
+            out.extend((np.concatenate([hi, hi], axis=0), lo))
+        elif k == 3:
+            out.extend((np.concatenate([hi, lo], axis=1), hi))
+        else:
+            out.extend((hi, lo))
     out.append(pairs.astype(np.float32).astype(jnp.bfloat16))
     out.append(x_twist.astype(np.float32))
     out.append(y_twist.astype(np.float32))
@@ -100,7 +106,9 @@
 
 
 def x_forward(phys, first, second, twist):
-    z = right_table(phys, first)
+    twice, lo = first
+    dh, dl = split(phys)
+    z = dot(jnp.concatenate([dh, dl], axis=1), twice) + dot(dh, lo)
     zr, zi = z[:, :LANES], z[:, LANES:]
     c, s = twist
     t = jnp.concatenate([zr * c + zi * s, zi * c - zr * s], axis=0)
@@ -112,8 +120,10 @@
     u = left_table(third, jnp.concatenate([re, im], axis=0))
     ur, ui = u[:256], u[256:]
     c, s = twist
-    t = jnp.concatenate([ur * c - ui * s, ur * s + ui * c], axis=1)
-    return right_table(t, last)
+    dh, dl = split(jnp.concatenate([ur * c - ui * s, ur * s + ui * c], axis=1))
+    both, hi = last
+    z = dot(dh, both)
+    return z[:, :LANES] + z[:, LANES:] + dot(dl, hi)
 
 
 def y_forward(re, im, first, second, twist):
@@ -148,17 +158,20 @@
 
 
 def get(buf, j, count):
-    return buf[:count, j, :]
+    rows, each = buf.shape[:2]
+    return buf.reshape(rows * each, LANES)[pl.ds(j, count, stride=each), :]
 
 
 def put(buf, j, value):
-    buf[: value.shape[0], j, :] = value
+    rows, each = buf.shape[:2]
+    buf.reshape(rows * each, LANES)[pl.ds(j, value.shape[0], stride=each), :] = value
 
 
 def far_first():
     hops = (0, 1, 2, 1)
     offsets = [(a, b, c) for a in range(4) for b in range(4) for c in range(4)]
-    return sorted(offsets, key=lambda o: -(hops[o[0]] + hops[o[1]] + hops[o[2]]))
+    weight = (0, 1.6, 2.6, 1)
+    return sorted(offsets, key=lambda o: -(weight[o[0]] + hops[o[1]] + hops[o[2]]))
 
 
 def surface_kernel(*refs):
@@ -264,7 +277,7 @@
 
     pl.semaphore_wait(barrier, COLS + ROWS - 2)
 
-    for f, ref in enumerate((phi_ref, eta_ref)):
+    def rows_to_lines(f, ref):
         for i in (5, 3, 7, 1, 4, 6, 2):
             to = (col + i) % COLS
             remote(
@@ -277,6 +290,9 @@
         pltpu.make_async_copy(
             ref.at[pl.ds(col * LINES, LINES), :], lines.at[f, col], recv_sems.at[f]
         ).start()
+
+    rows_to_lines(0, phi_ref)
+    rows_to_lines(1, eta_ref)
 
     x_at = (col % 2) * 2 + row // 8
     y_at = (row // 2) % 4
@@ -565,12 +581,14 @@
     eta = fields[1]
     fields[2] = fields[2] + eta * (fields[3] + curve_two) + 0.5 * eta * eta * cube_one
 
+    out_t[4] = jnp.transpose(eta)
+    coarse_t[3] = coarsen(4)
+
     wait_bytes(recv6.at[:OWNERS], recv_sems.at[11])
     height_rate = fields[8] + fields[7] * (fields[2] + inverse_x(recv6, 0))
     out_t[3] = jnp.transpose(height_rate)
     spread(0, fine(3), height_out.at[my_fine, :])
-    out_t[4] = jnp.transpose(GRAVITY * (fields[1] + SURFACE_STEP * height_rate))
-    pressure = coarsen(4)
+    pressure = GRAVITY * (coarse_t[3] + SURFACE_STEP * coarsen(3))
     coarse_t[2] = pressure
     spread(5, few(2), press_out.at[pl.ds(col * 8 + 8, 8), :])
 

time: 65 us -> 64.1 us (0.986)
  Pallas kernels: 64.3 us -> 63.4 us
    pallas_call x1, Pallas kernels: 63 us -> 62.1 us  [local(): pl.pallas_call(surface_kernel, name='surface', out_shape=[shape(128, 256)...]
where the time goes in v4:
time: 64.1 us; the launch traced here: 64 us
  Pallas kernels  63.4 us (99%)
    pallas_call x1, Pallas kernels, local(): pl.pallas_call(surface_kernel, name='surface', out_shape=[shape(128, 256)...  62.1 us

profile of v4, /device:TPU:1, one launch (start us, length us, event | category | flops | bytes accessed | tf_op | source)
XLA Modules:
  0.0 64.0 jit_solution(4209653492545202067)
XLA Ops:
  0.6 62.1 %surface.1 = (f32[128,256]{1,0:T(8,128)S(1)}, f32[64,128]{1,0:T(8,128)S(1)}, f32[80,128]{1,0:T(8,128)S(1)}, f32[48,64,128]{2,1,0:T(8,128)S(1)}, f32[128,256]{1,0...) custom-call(f32[128,256]{1,0:T(8,128)} %refs_0_.1, f32[128,256]{1,0:T(8,128)} %refs_1_.1, ...), custom_call_target="tpu_custom_call" | custom-call | tf_op jit(solution)/shard_map/surface/pallas_call | solution.py:717
  62.7 1.3 %load.1 = (f32[48,64,128]{2,1,0:T(8,128)}, f32[128,256]{1,0:T(8,128)}, f32[128,256]{1,0:T(8,128)}) custom-call(f32[64,128]{1,0:T(8,128)S(1)} %get-tuple-element.13.refs_0_, f32[80,128]{1,0:T(8,128)S(1)} %get-tuple-element.14.refs_1_, f32[128,256]{1,0:T(8,128)S(1)} %get-tuple-element.15.refs_2_, f32[128,256]{1,0:T(8,128)S(1)} %get-tuple-element.16.refs_3_, ...), custom_call_target="tpu_custom_call" | custom-call | tf_op jit(solution)/shard_map/load/pallas_call | solution.py:763

commit v5 on v4

--- a/solution.py
+++ b/solution.py
@@ -24,7 +24,7 @@
 VISCOSITY = 0.2
 DECAY_RATE = 0.05
 LOGICAL = pl.DeviceIdType.LOGICAL
-EARLY_LEVELS = 12
+EARLY_LEVELS = 8
 SURFACE_VMEM = 20 * 1024 * 1024
 LOAD_VMEM = 8 * 1024 * 1024
 F32 = jnp.float32
@@ -486,8 +486,6 @@
     my_few, my_fine = pl.ds(col * 8, 8), pl.ds(col * LINES, LINES)
     spread(2, few(0), su_tile.at[my_few, :])
     spread(3, few(1), sv_tile.at[my_few, :])
-    fields[7] = inverse_x(recv2c, 2)
-    fields[8] = inverse_x(recv2c, 3)
 
     wait_bytes(recv4.at[:OWNERS], recv_sems.at[8])
     vert_two = inverse_x(recv4, 0)
@@ -500,7 +498,8 @@
     def _():
         to_lines(send2d, recv2d, 12)
 
-    pot_dx, pot_dy, height_dx, height_dy = (fields[5 + j] for j in range(4))
+    pot_dx, pot_dy = fields[5], fields[6]
+    height_dx, height_dy = inverse_x(recv2c, 2), inverse_x(recv2c, 3)
     stretch = 1.0 + (height_dx * height_dx + height_dy * height_dy)
     advected = -(height_dx * pot_dx + height_dy * pot_dy)
     fields[7] = stretch

time: 64.1 us -> 64 us (level)
  no operation moved by 1% of the time
where the time goes in v5:
time: 64 us; the launch traced here: 63.9 us
  Pallas kernels  63.3 us (99%)
  between operations  0.64 us (1%)
    pallas_call x1, Pallas kernels, local(): pl.pallas_call(surface_kernel, name='surface', out_shape=[shape(128, 256)...  62 us
    pallas_call x1, Pallas kernels, local(): pl.pallas_call(load_kernel, name='load', out_shape=[shape(3 * LZ, 64, LAN...  1.28 us

profile of v5, /device:TPU:1, one launch (start us, length us, event | category | flops | bytes accessed | tf_op | source)
XLA Modules:
  0.0 63.9 jit_solution(342340131829013503)
XLA Ops:
  0.6 62.0 %surface.1 = (f32[128,256]{1,0:T(8,128)S(1)}, f32[64,128]{1,0:T(8,128)S(1)}, f32[80,128]{1,0:T(8,128)S(1)}, f32[48,64,128]{2,1,0:T(8,128)S(1)}, f32[128,256]{1,0...) custom-call(f32[128,256]{1,0:T(8,128)} %refs_0_.1, f32[128,256]{1,0:T(8,128)} %refs_1_.1, ...), custom_call_target="tpu_custom_call" | custom-call | tf_op jit(solution)/shard_map/surface/pallas_call | solution.py:716
  62.6 1.3 %load.1 = (f32[48,64,128]{2,1,0:T(8,128)}, f32[128,256]{1,0:T(8,128)}, f32[128,256]{1,0:T(8,128)}) custom-call(f32[64,128]{1,0:T(8,128)S(1)} %get-tuple-element.13.refs_0_, f32[80,128]{1,0:T(8,128)S(1)} %get-tuple-element.14.refs_1_, f32[128,256]{1,0:T(8,128)S(1)} %get-tuple-element.15.refs_2_, f32[128,256]{1,0:T(8,128)S(1)} %get-tuple-element.16.refs_3_, ...), custom_call_target="tpu_custom_call" | custom-call | tf_op jit(solution)/shard_map/load/pallas_call | solution.py:762

commit v6 on v5

--- a/solution.py
+++ b/solution.py
@@ -324,7 +324,7 @@
             ).start()
             return 0
 
-        lax.fori_loop(0, OWNERS - 1, step, 0, unroll=5)
+        lax.fori_loop(0, OWNERS - 1, step, 0, unroll=17)
 
         @pl.when(is_owner)
         def _():
@@ -342,7 +342,7 @@
             ).start()
             return 0
 
-        lax.fori_loop(0, DEVS - 2, step, 0, unroll=6)
+        lax.fori_loop(0, DEVS - 2, step, 0, unroll=18)
         step(DEVS - 2, 0)
         pltpu.make_async_copy(send.at[me], recv.at[my_p], recv_sems.at[k]).start()
 
@@ -428,8 +428,6 @@
         spec[3] = im * weight
         inverse_y(-kx * spec[3], kx * spec[2], send2c, 2)
         inverse_y(-ky * spec[3], ky * spec[2], send2c, 3)
-        cube = square * mag
-        inverse_y(spec[0] * cube, spec[1] * cube, send2d, 0)
 
     wait_bytes(recv2.at[:OWNERS], recv_sems.at[4])
     vert = inverse_x(recv2, 0)
@@ -440,6 +438,9 @@
     @pl.when(is_owner)
     def _():
         to_lines(send2c, recv2c, 6)
+        kx, ky, mag, weight = wave_grids(my_p)
+        cube = mag * mag * mag
+        inverse_y(spec[0] * cube, spec[1] * cube, send2d, 0)
 
     wait_bytes(recv2b.at[:OWNERS], recv_sems.at[5])
     fields[3] = inverse_x(recv2b, 0)

time: 64 us -> 64 us (level)
  no operation moved by 1% of the time
where the time goes in v6:
time: 64 us; the launch traced here: 63.9 us
  Pallas kernels  63.2 us (99%)
  between operations  0.64 us (1%)
    pallas_call x1, Pallas kernels, local(): pl.pallas_call(surface_kernel, name='surface', out_shape=[shape(128, 256)...  62 us
    pallas_call x1, Pallas kernels, local(): pl.pallas_call(load_kernel, name='load', out_shape=[shape(3 * LZ, 64, LAN...  1.28 us

profile of v6, /device:TPU:1, one launch (start us, length us, event | category | flops | bytes accessed | tf_op | source)
XLA Modules:
  0.0 63.9 jit_solution(2363858246482398641)
XLA Ops:
  0.6 62.0 %surface.1 = (f32[128,256]{1,0:T(8,128)S(1)}, f32[64,128]{1,0:T(8,128)S(1)}, f32[80,128]{1,0:T(8,128)S(1)}, f32[48,64,128]{2,1,0:T(8,128)S(1)}, f32[128,256]{1,0...) custom-call(f32[128,256]{1,0:T(8,128)} %refs_0_.1, f32[128,256]{1,0:T(8,128)} %refs_1_.1, ...), custom_call_target="tpu_custom_call" | custom-call | tf_op jit(solution)/shard_map/surface/pallas_call | solution.py:717
  62.6 1.3 %load.1 = (f32[48,64,128]{2,1,0:T(8,128)}, f32[128,256]{1,0:T(8,128)}, f32[128,256]{1,0:T(8,128)}) custom-call(f32[64,128]{1,0:T(8,128)S(1)} %get-tuple-element.13.refs_0_, f32[80,128]{1,0:T(8,128)S(1)} %get-tuple-element.14.refs_1_, f32[128,256]{1,0:T(8,128)S(1)} %get-tuple-element.15.refs_2_, f32[128,256]{1,0:T(8,128)S(1)} %get-tuple-element.16.refs_3_, ...), custom_call_target="tpu_custom_call" | custom-call | tf_op jit(solution)/shard_map/load/pallas_call | solution.py:763
